TPU v7x, 32 devices: a whole 2x2x4 slice. The times are simulated.
32 devices in a mesh: lon: 8 (over z, x), lat: 4 (over y, core).
Axes of the slice: x: 2, y: 2, z: 4, core: 2. Of those that a mesh axis runs over, the one named last changes fastest.
Arguments:
- inputs: bfloat16 [256, 32, 2048], P(None, 'lat', 'lon'), may hold values from -6 to 6
- cotangent: bfloat16 [256, 32, 2048], P(None, 'lat', 'lon'), may hold values from -6 to 6
- mixing: bfloat16 [9, 256, 256], replicated, may hold values from -0.125 to 0.125
- filters: bfloat16 [9, 32, 3, 33], P(None, 'lat'), may hold values from -0.8984375 to 0.8984375
- support: int32 [32], P('lat'), may hold values from 1 to 16, as said below
Outputs:
- input_grad: bfloat16 [256, 32, 2048], P(None, 'lat', 'lon')
- weight_grad: float32 [9, 256, 256], replicated
Inputs may be any that keep to these rules, and one draw needn't show every extreme that they name: support[i] is the widest longitude offset, in cells, reached by the filter of latitude row i.
All inputs are finite; a program needn't handle non-finite values.
Results may differ from a plain program's by a relative error of at most 0.0051.
Values may be sent and summed in bfloat16 or wider, within the bound.
A program may use at most 192 MiB of HBM per device.

v0:
```python
import math

import jax
import jax.numpy as jnp
from jax import lax
from jax.sharding import PartitionSpec as P

LAT_REACH = 1
LON_REACH = 16


def with_halo(cells, sides, width, closed):
    for axis, dim in sides:
        count = lax.axis_size(axis)
        ends = count if closed else count - 1
        head = lax.slice_in_dim(cells, 0, width, axis=dim)
        tail = lax.slice_in_dim(cells, cells.shape[dim] - width, cells.shape[dim], axis=dim)
        cells = jnp.concatenate(
            [
                lax.ppermute(tail, axis, [(i, (i + 1) % count) for i in range(ends)]),
                cells,
                lax.ppermute(head, axis, [((i + 1) % count, i) for i in range(ends)]),
            ],
            axis=dim,
        )
    return cells


def spread_block(source, coef_source, row_first, rows, col_first, cols):
    kernels = coef_source.shape[0]
    chans = source.shape[0]
    span = LON_REACH
    reach = LAT_REACH
    tap_count = 2 * span + 1
    window = cols + 2 * span
    tap_axis = jnp.arange(tap_count, dtype=jnp.int32)[:, None, None]
    wide_axis = jnp.arange(window, dtype=jnp.int32)[None, :, None]
    cell_axis = jnp.arange(cols, dtype=jnp.int32)[None, None, :]
    selector = (cell_axis + 2 * span - wide_axis == tap_axis).astype(jnp.bfloat16)
    total = jnp.zeros((kernels, chans, rows, cols), jnp.float32)
    for offset in range(2 * reach + 1):
        start = row_first + 2 * reach - offset
        rows_in = source[:, start : start + rows, col_first : col_first + window]
        part_coefs = coef_source[:, start : start + rows, offset, :]
        tiles = jnp.einsum(
            "bpq,kib->kipq", selector, part_coefs, preferred_element_type=jnp.float32
        ).astype(jnp.bfloat16)
        total = total + jnp.einsum(
            "oip,kipq->koiq", rows_in, tiles, preferred_element_type=jnp.float32
        )
    return total.astype(jnp.bfloat16)


def local(inputs, cotangent, mixing, filters, support):
    chans, lat_rows, lon_cols = inputs.shape
    span = LON_REACH
    reach = LAT_REACH
    tap_count = 2 * span + 1
    offsets = jnp.arange(tap_count, dtype=jnp.int32) - span
    keep = (jnp.abs(offsets)[None, :] <= support[:, None]).astype(jnp.bfloat16)
    coefs = filters * keep[None, :, None, :]
    widened = with_halo(cotangent, (("lon", 2),), span, True)
    padded = with_halo(widened, (("lat", 1),), reach, False)
    coef_pad = with_halo(coefs, (("lat", 1),), reach, False)
    spread = spread_block(padded, coef_pad, 0, lat_rows, 0, lon_cols)
    local_grad = jnp.einsum("koiq,ciq->koc", spread, inputs, preferred_element_type=jnp.float32)
    total_cells = lat_rows * lax.axis_size("lat") * lon_cols * lax.axis_size("lon")
    weight_grad = lax.psum(local_grad, ("lon", "lat")) * (1.0 / math.sqrt(total_cells))
    input_grad = jnp.einsum(
        "koc,koiq->ciq", mixing, spread, preferred_element_type=jnp.float32
    ).astype(jnp.bfloat16)
    return (input_grad, weight_grad)


def solution(mesh):
    return jax.shard_map(
        local,
        mesh=mesh,
        in_specs=(
            P(None, "lat", "lon"),
            P(None, "lat", "lon"),
            P(),
            P(None, "lat", None, None),
            P("lat"),
        ),
        out_specs=(P(None, "lat", "lon"), P()),
        check_vma=False,
    )
```

profile of v0, /device:TPU:0, one launch (start us, length us, event | category | flops | bytes accessed | tf_op | source)
XLA Modules:
  0.0 247.0 jit_solution(17493707170582099157)
XLA Ops:
  7.2 0.0 copy-start
  7.2 0.0 copy-start.2
  7.2 0.0 copy-start.1
  7.2 0.0 all-reduce.2.cloned.1.call-start
  7.2 1.7 copy.7
  9.0 3.0 %collective-permute-start.1 = (bf16[256,8,16]{0,2,1:T(8,128)(2,1)S(1)}, bf16[256,8,16]{0,2,1:T(8,128)(2,1)S(1)}, u32[]{:S(2)}, u32[]{:S(2)}) collective-permute-start(bf16[256,8,16]{0,2,1:T(8,128)(2,1)S(1)} %get-tuple-element.6), channel_id=1, source_target_pairs={{0,4},{4,8},{8,12},{12,16},{16,20},{20,24},{24,28},{28,0},{1,5},{5... | collective-permute-start | bytes 196616 | tf_op jit(solution)/shard_map/ppermute | solution.py:20
  12.0 3.1 %collective-permute-start.2 = (bf16[256,8,16]{0,2,1:T(8,128)(2,1)S(1)}, bf16[256,8,16]{0,2,1:T(8,128)(2,1)S(1)}, u32[]{:S(2)}, u32[]{:S(2)}) collective-permute-start(bf16[256,8,16]{0,2,1:T(8,128)(2,1)S(1)} %get-tuple-element.7), channel_id=1, source_target_pairs={{4,0},{8,4},{12,8},{16,12},{20,16},{24,20},{28,24},{0,28},{5,1},{9... | collective-permute-start | bytes 196616 | tf_op jit(solution)/shard_map/ppermute | solution.py:22
  15.1 0.0 copy-done.2
  15.1 0.1 compare_convert_fusion
  15.2 0.0 copy-done.1
  15.2 1.3 collective-permute-start
  16.5 3.0 %collective-permute-start.4 = (bf16[9,1,3,33]{3,1,2,0:T(2,128)(2,1)S(1)}, bf16[9,1,3,33]{3,1,2,0:T(2,128)(2,1)S(1)}, u32[]{:S(2)}, u32[]{:S(2)}) collective-permute-start(bf16[9,1,3,33]{3,1,2,0:T(2,128)(2,1)S(1)} %get-tuple-element.8), channel_id=1, source_target_pairs={{0,1},{1,2},{2,3},{4,5},{5,6},{6,7},{8,9},{9,10},{10,11},{12,13},{... | collective-permute-start | bytes 5354 | tf_op jit(solution)/shard_map/ppermute | solution.py:20
  19.6 1.3 fusion.3
  20.9 6.6 %fusion.7 = bf16[9,8,288,256]{3,1,2,0:T(8,128)(2,1)} fusion(pred[33,288,256,1]{2,1,0,3:T(32,128)(4,1)S(1)} %fusion.3, bf16[9,8,3,33]{3,1,2,0:T(8,128)(2,1)S(1)} %broadcast_multiply_fusion.1), kind=kOutput, calls=%fused_computation.12 | convolution fusion | flops 350355456 | bytes 13068288 | tf_op jit(solution)/shard_map/bpq,kib->kipq/dot_general | solution.py:45
  27.5 0.0 collective-permute-done
  27.5 6.6 %fusion.9 = bf16[9,8,288,256]{3,1,2,0:T(8,128)(2,1)} fusion(pred[33,288,256,1]{2,1,0,3:T(32,128)(4,1)S(1)} %fusion.3, bf16[9,1,3,33]{3,1,2,0:T(2,128)(2,1)S(1)} %collective-permute-done, bf16[9,8,3,33]{3,1,2,0:T(8,128)(2,1)S(1)} %broadcast_multiply_fusion.1), kind=kOutput, calls=%fused_computation.14 | convolution fusion | flops 350364960 | bytes 13065894 | tf_op jit(solution)/shard_map/bpq,kib->kipq/dot_general | solution.py:45
  34.1 0.0 collective-permute-done.4
  34.1 6.6 %fusion.5 = bf16[9,8,288,256]{3,1,2,0:T(8,128)(2,1)} fusion(pred[33,288,256,1]{2,1,0,3:T(32,128)(4,1)S(1)} %fusion.3, bf16[9,8,3,33]{3,1,2,0:T(8,128)(2,1)S(1)} %broadcast_multiply_fusion.1, bf16[9,1,3,33]{3,1,2,0:T(2,128)(2,1)S(1)} %collective-permute-done.4), kind=kOutput, calls=%fused_computation.10 | convolution fusion | flops 350364960 | bytes 13065894 | tf_op jit(solution)/shard_map/bpq,kib->kipq/dot_general | solution.py:45
  40.7 0.0 collective-permute-done.1
  40.7 0.0 collective-permute-done.2
  40.7 0.1 pad_maximum_fusion.10
  40.8 0.0 slice-start
  40.8 0.7 fusion.31
  41.5 1.4 collective-permute-start.3
  42.9 0.0 slice-start.1
  43.0 0.0 slice-start.2
  43.0 4.7 %collective-permute-start.5 = (bf16[256,1,288]{0,2,1:T(8,128)(2,1)}, bf16[256,1,288]{0,2,1:T(8,128)(2,1)}, u32[]{:S(2)}, u32[]{:S(2)}) collective-permute-start(bf16[256,1,288]{0,2,1:T(8,128)(2,1)} %get-tuple-element.4), channel_id=1, source_target_pairs={{0,1},{1,2},{2,3},{4,5},{5,6},{6,7},{8,9},{9,10},{10,11},{12,13},{... | collective-permute-start | bytes 442376 | tf_op jit(solution)/shard_map/ppermute | solution.py:20
  47.7 12.9 %fusion.1 = f32[8,9,256,256]{3,2,1,0:T(8,128)} fusion(bf16[9,8,288,256]{3,1,2,0:T(8,128)(2,1)} %fusion.7, bf16[256,8,16]{0,2,1:T(8,128)(2,1)S(1)} %collective-permute-done.2, bf16[256,8,256]{0,2,1:T(8,128)(2,1)S(1)} %copy.7, bf16[256,8,16]{0,2,1:T(8,128)(2,1)S(1)} %collective-permute-done.1), kind=kOutput, calls=%fused_computation.5 | convolution fusion | flops 2721447936 | bytes 30670848 | tf_op jit(solution)/shard_map/oip,kipq->koiq/dot_general | solution.py:48
  60.6 0.0 collective-permute-done.3
  60.6 0.0 slice-done
  60.6 0.0 slice-done.1
  60.6 0.0 slice-done.2
  60.6 12.4 %fusion = f32[8,9,256,256]{3,2,1,0:T(8,128)} fusion(bf16[9,8,288,256]{3,1,2,0:T(8,128)(2,1)S(1)} %bitcast.53, bf16[256,1,288]{0,2,1:T(8,128)(2,1)} %collective-permute-done.3, bf16[256,8,16]{0,2,1:T(8,128)(2,1)S(1)} %collective-permute-done.2, bf16[256,8,256]{0,2,1:T(8,128)(2,1)S(1)} %copy.7, bf16[256,8,16]{0,2,1:T(8,128)(2,1)S(1)} %collective-permute-done.1), kind=kOutput, calls=%fused_computation.4 | convolution fusion | flops 2722627584 | bytes 30818304 | tf_op jit(solution)/shard_map/oip,kipq->koiq/dot_general | solution.py:48
  73.0 0.0 copy-start.3
  73.0 0.0 collective-permute-done.5
  73.0 21.8 %fusion.4 = bf16[9,256,8,256]{1,3,0,2:T(8,128)(2,1)} fusion(f32[8,9,256,256]{3,2,1,0:T(8,128)} %fusion, f32[8,9,256,256]{3,2,1,0:T(8,128)} %fusion.1, bf16[9,8,288,256]{3,1,2,0:T(8,128)(2,1)} %fusion.5, bf16[256,1,288]{0,2,1:T(8,128)(2,1)} %collective-permute-done.5, bf16[256,8,16]{0,2,1:T(8,128)(2,1)S(1)} %collective-permute-done.2, ...), kind=kOutput, calls=%fused_computation.9 | convolution fusion | flops 2736783360 | bytes 59129856 | tf_op jit(solution)/shard_map/oip,kipq->koiq/dot_general | solution.py:48
  94.8 0.0 copy-done.3
  94.8 7.8 %convolution_bitcast_fusion = f32[9,256,256]{2,1,0:T(8,128)} fusion(bf16[9,256,8,256]{1,3,0,2:T(8,128)(2,1)} %fusion.4, bf16[256,8,256,1]{2,1,0,3:T(8,128)(2,1)S(1)} %bitcast.54), kind=kOutput, calls=%fused_computation.17 | convolution fusion | flops 2415919104 | bytes 12845056 | tf_op jit(solution)/shard_map/koiq,ciq->koc/dot_general | solution.py:66
  102.6 0.0 all-reduce.2.cloned.1.call-update
  102.6 0.0 copy-done
  102.6 6.3 %fusion.11 = bf16[256,8,256]{0,2,1:T(8,128)(2,1)S(1)} fusion(bf16[9,256,8,256]{1,3,0,2:T(8,128)(2,1)} %fusion.4, bf16[9,256,256]{2,1,0:T(8,128)(2,1)S(1)} %copy-done), kind=kOutput, calls=%fused_computation.18 | convolution fusion | flops 2416443392 | bytes 11665408 | tf_op jit(solution)/shard_map/koc,koiq->ciq/dot_general | solution.py:69
  109.0 1.8 copy.12
  110.8 126.1 %all-reduce.2.cloned.1.call-done = f32[9,256,256]{2,1,0:T(8,128)} async-done(((f32[9,256,256]{2,1,0:T(8,128)}), f32[9,256,256]{2,1,0:T(8,128)}) %all-reduce.2.cloned.1.call-update) | async-done | bytes 2359312 | tf_op jit(solution)/shard_map/psum | solution.py:68
  236.8 3.3 %broadcast_multiply_fusion = f32[9,256,256]{2,1,0:T(8,128)} fusion(f32[9,256,256]{2,1,0:T(8,128)} %all-reduce.2.cloned.1.call-done), kind=kLoop, calls=%fused_computation.32 | loop fusion | flops 589824 | bytes 4718592 | tf_op jit(solution)/shard_map/mul | solution.py:68
  (7 shorter events, 0.1 us)
Async XLA Ops:
  7.2 95.5 %copy-start = (bf16[9,256,256]{2,1,0:T(8,128)(2,1)S(1)}, bf16[9,256,256]{2,1,0:T(8,128)(2,1)}, u32[]{:S(2)}) copy-start(bf16[9,256,256]{2,1,0:T(8,128)(2,1)} %param.7) | copy-start | bytes 3538948
  7.2 7.9 %copy-start.2 = (s32[8]{0:T(128)S(1)}, s32[8]{0:T(128)}, u32[]{:S(2)}) copy-start(s32[8]{0:T(128)} %param.9) | copy-start | bytes 100
  7.2 8.0 %copy-start.1 = (bf16[9,8,3,33]{3,1,2,0:T(8,128)(2,1)S(1)}, bf16[9,8,3,33]{3,1,2,0:T(8,128)(2,1)}, u32[]{:S(2)}) copy-start(bf16[9,8,3,33]{3,1,2,0:T(8,128)(2,1)} %param.8) | copy-start | bytes 42772
  7.2 229.6 %all-reduce.2.cloned.1.call-start = ((), (), s32[]{:S(2)}) async-start(), calls=%async_computation | async-start | bytes 4718592 | tf_op jit(solution)/shard_map/psum | solution.py:68
  9.0 31.7 %collective-permute-start.1 = (bf16[256,8,16]{0,2,1:T(8,128)(2,1)S(1)}, bf16[256,8,16]{0,2,1:T(8,128)(2,1)S(1)}, u32[]{:S(2)}, u32[]{:S(2)}) collective-permute-start(bf16[256,8,16]{0,2,1:T(8,128)(2,1)S(1)} %get-tuple-element.6), channel_id=1, source_target_pairs={{0,4},{4,8},{8,12},{12,16},{16,20},{20,24},{24,28},{28,0},{1,5},{5... | collective-permute-start | bytes 196616 | tf_op jit(solution)/shard_map/ppermute | solution.py:20
  12.0 28.7 %collective-permute-start.2 = (bf16[256,8,16]{0,2,1:T(8,128)(2,1)S(1)}, bf16[256,8,16]{0,2,1:T(8,128)(2,1)S(1)}, u32[]{:S(2)}, u32[]{:S(2)}) collective-permute-start(bf16[256,8,16]{0,2,1:T(8,128)(2,1)S(1)} %get-tuple-element.7), channel_id=1, source_target_pairs={{4,0},{8,4},{12,8},{16,12},{20,16},{24,20},{28,24},{0,28},{5,1},{9... | collective-permute-start | bytes 196616 | tf_op jit(solution)/shard_map/ppermute | solution.py:22
  15.2 12.3 %collective-permute-start = (bf16[9,1,3,33]{3,1,2,0:T(2,128)(2,1)S(1)}, bf16[9,1,3,33]{3,1,2,0:T(2,128)(2,1)S(1)}, u32[]{:S(2)}, u32[]{:S(2)}) collective-permute-start(bf16[9,1,3,33]{3,1,2,0:T(2,128)(2,1)S(1)} %get-tuple-element.9), channel_id=1, source_target_pairs={{1,0},{2,1},{3,2},{5,4},{6,5},{7,6},{9,8},{10,9},{11,10},{13,12},{... | collective-permute-start | bytes 5354 | tf_op jit(solution)/shard_map/ppermute | solution.py:22
  16.5 17.5 %collective-permute-start.4 = (bf16[9,1,3,33]{3,1,2,0:T(2,128)(2,1)S(1)}, bf16[9,1,3,33]{3,1,2,0:T(2,128)(2,1)S(1)}, u32[]{:S(2)}, u32[]{:S(2)}) collective-permute-start(bf16[9,1,3,33]{3,1,2,0:T(2,128)(2,1)S(1)} %get-tuple-element.8), channel_id=1, source_target_pairs={{0,1},{1,2},{2,3},{4,5},{5,6},{6,7},{8,9},{9,10},{10,11},{12,13},{... | collective-permute-start | bytes 5354 | tf_op jit(solution)/shard_map/ppermute | solution.py:20
  40.8 19.8 %slice-start = ((s8[10616832]{0:T(1024)(128)(4,1)}), s8[4194304]{0:T(1024)(128)(4,1)S(1)}, s32[]{:S(2)}) async-start(s8[10616832]{0:T(1024)(128)(4,1)} %bitcast.52), calls=%async_computation.1 | async-start | bytes 8388608
  41.5 19.1 %collective-permute-start.3 = (bf16[256,1,288]{0,2,1:T(8,128)(2,1)}, bf16[256,1,288]{0,2,1:T(8,128)(2,1)}, u32[]{:S(2)}, u32[]{:S(2)}) collective-permute-start(bf16[256,1,288]{0,2,1:T(8,128)(2,1)} %get-tuple-element.5), channel_id=1, source_target_pairs={{1,0},{2,1},{3,2},{5,4},{6,5},{7,6},{9,8},{10,9},{11,10},{13,12},{... | collective-permute-start | bytes 442376 | tf_op jit(solution)/shard_map/ppermute | solution.py:22
  42.9 17.7 %slice-start.1 = ((s8[10616832]{0:T(1024)(128)(4,1)}), s8[4194304]{0:T(1024)(128)(4,1)S(1)}, s32[]{:S(2)}) async-start(s8[10616832]{0:T(1024)(128)(4,1)} %bitcast.52), calls=%async_computation.2 | async-start | bytes 8388608
  43.0 17.7 %slice-start.2 = ((s8[10616832]{0:T(1024)(128)(4,1)}), s8[2228224]{0:T(1024)(128)(4,1)S(1)}, s32[]{:S(2)}) async-start(s8[10616832]{0:T(1024)(128)(4,1)} %bitcast.52), calls=%async_computation.3 | async-start | bytes 4456448
  43.0 30.1 %collective-permute-start.5 = (bf16[256,1,288]{0,2,1:T(8,128)(2,1)}, bf16[256,1,288]{0,2,1:T(8,128)(2,1)}, u32[]{:S(2)}, u32[]{:S(2)}) collective-permute-start(bf16[256,1,288]{0,2,1:T(8,128)(2,1)} %get-tuple-element.4), channel_id=1, source_target_pairs={{0,1},{1,2},{2,3},{4,5},{5,6},{6,7},{8,9},{9,10},{10,11},{12,13},{... | collective-permute-start | bytes 442376 | tf_op jit(solution)/shard_map/ppermute | solution.py:20
  73.0 21.8 %copy-start.3 = (bf16[256,8,256]{2,1,0:T(8,128)(2,1)S(1)}, bf16[256,8,256]{2,1,0:T(8,128)(2,1)}, u32[]{:S(2)}) copy-start(bf16[256,8,256]{2,1,0:T(8,128)(2,1)} %param.5) | copy-start | bytes 3145732
Sparse Core Ops, SparseCore 0:
  102.8 134.0 all-reduce.1
where the time goes:
time: 247 us
  waiting for transfers between devices  126 us (51%)
  matrix products  81 us (33%)
  starting transfers between devices  16.6 us (7%)
  between operations  14.2 us (6%)
  other arithmetic  4.73 us (2%)
  local copies, waits for them, and re-layouts  4.31 us (2%)
    psum x1, waiting for transfers between devices, local(): lax.psum(local_grad, ('lon', 'lat')) * (1.0 / math.sqrt(total_cells))  126 us
    dot_general x3, matrix products, spread_block(): jnp.einsum('oip,kipq->koiq', rows_in, tiles, preferred_element_type=jnp.f...  47.1 us
    dot_general x3, matrix products, spread_block(): jnp.einsum('bpq,kib->kipq', selector, part_coefs, preferred_element_type=...  19.8 us
    ppermute x3, starting transfers between devices, with_halo(): lax.ppermute(tail, axis, [(i, (i + 1) % count) for i in range(ends)])  10.8 us
    dot_general x1, matrix products, local(): jnp.einsum('koiq,ciq->koc', spread, inputs, preferred_element_type=jnp.fl...  7.76 us
    dot_general x1, matrix products, local(): jnp.einsum('koc,koiq->ciq', mixing, spread, preferred_element_type=jnp.fl...  6.3 us
    ppermute x3, starting transfers between devices, with_halo(): lax.ppermute(head, axis, [((i + 1) % count, i) for i in range(ends)])  5.81 us
  transfers between devices with their start and end apart: 7, of which 1 were waited for; matrix products, arithmetic and copies ran while one was open for 22% of the time, Pallas kernels for 0%

commit v1 on v0

--- a/solution.py
+++ b/solution.py
@@ -24,6 +24,34 @@
             axis=dim,
         )
     return cells
+
+
+def halving_psum(x):
+    stages = []
+    for axis in ("lat", "lon"):
+        bit = 1
+        while bit < lax.axis_size(axis):
+            stages.append((axis, bit))
+            bit *= 2
+    cur = x.reshape(-1, x.shape[-1])
+    if cur.shape[0] % (2 ** len(stages)):
+        return lax.psum(x, ("lon", "lat"))
+    for axis, bit in stages:
+        count = lax.axis_size(axis)
+        side = (lax.axis_index(axis) // bit) % 2
+        half = cur.shape[0] // 2
+        keep = lax.dynamic_slice_in_dim(cur, side * half, half, 0)
+        send = lax.dynamic_slice_in_dim(cur, (1 - side) * half, half, 0)
+        cur = keep + lax.ppermute(send, axis, [(i, i ^ bit) for i in range(count)])
+    for axis, bit in reversed(stages):
+        count = lax.axis_size(axis)
+        side = (lax.axis_index(axis) // bit) % 2
+        other = lax.ppermute(cur, axis, [(i, i ^ bit) for i in range(count)])
+        half = cur.shape[0]
+        buf = jnp.zeros((2 * half, cur.shape[1]), cur.dtype)
+        buf = lax.dynamic_update_slice_in_dim(buf, cur, side * half, 0)
+        cur = lax.dynamic_update_slice_in_dim(buf, other, (1 - side) * half, 0)
+    return cur.reshape(x.shape)
 
 
 def spread_block(source, coef_source, row_first, rows, col_first, cols):
@@ -65,7 +93,7 @@
     spread = spread_block(padded, coef_pad, 0, lat_rows, 0, lon_cols)
     local_grad = jnp.einsum("koiq,ciq->koc", spread, inputs, preferred_element_type=jnp.float32)
     total_cells = lat_rows * lax.axis_size("lat") * lon_cols * lax.axis_size("lon")
-    weight_grad = lax.psum(local_grad, ("lon", "lat")) * (1.0 / math.sqrt(total_cells))
+    weight_grad = halving_psum(local_grad) * (1.0 / math.sqrt(total_cells))
     input_grad = jnp.einsum(
         "koc,koiq->ciq", mixing, spread, preferred_element_type=jnp.float32
     ).astype(jnp.bfloat16)

time: 247 us -> 180 us (0.73)
  waiting for transfers between devices: 126 us -> 56.4 us
  between operations: 14.2 us -> 1.07 us
  starting transfers between devices: 16.6 us -> 26.7 us
  local copies, waits for them, and re-layouts: 4.31 us -> 7.3 us
    psum x1 -> x0, waiting for transfers between devices: 126 us -> none  [local(): lax.psum(local_grad, ('lon', 'lat')) * (1.0 / math.sqrt(total_cells))]
    ppermute x0 -> x10, waiting for transfers between devices: none -> 56.3 us  [the longest x5 35.1 us: halving_psum(): cur = keep + lax.ppermute(send, axis, [(i, i ^ bit) for i in range(count)])]
    ppermute x0 -> x10, starting transfers between devices: none -> 10.3 us  [the longest x5 6.21 us: halving_psum(): other = lax.ppermute(cur, axis, [(i, i ^ bit) for i in range(count)])]
    ppermute x3, starting transfers between devices: 10.8 us -> 7.63 us  [with_halo(): lax.ppermute(tail, axis, [(i, (i + 1) % count) for i in range(ends)])]
    ppermute x3, starting transfers between devices: 5.81 us -> 8.76 us  [with_halo(): lax.ppermute(head, axis, [((i + 1) % count, i) for i in range(ends)])]
    unnamed x16 -> x18, local copies, waits for them, and re-layouts: 3.54 us -> 5.7 us
  transfers between devices with their start and end apart: 7 -> 16, of which waited for: 1 -> 9; matrix products, arithmetic and copies ran while one was open for 22% -> 34% of each run, Pallas kernels for 0% -> 0%
where the time goes in v1:
time: 180 us; the launch traced here: 179 us
  matrix products  81.8 us (45%)
  waiting for transfers between devices  56.4 us (31%)
  starting transfers between devices  26.7 us (15%)
  local copies, waits for them, and re-layouts  7.3 us (4%)
  other arithmetic  6.15 us (3%)
    dot_general x3, matrix products, spread_block(): jnp.einsum('oip,kipq->koiq', rows_in, tiles, preferred_element_type=jnp.f...  47.2 us
    ppermute x5, waiting for transfers between devices, halving_psum(): cur = keep + lax.ppermute(send, axis, [(i, i ^ bit) for i in range(count)])  35.1 us
    dot_general x3, matrix products, spread_block(): jnp.einsum('bpq,kib->kipq', selector, part_coefs, preferred_element_type=...  21.8 us
    ppermute x5, waiting for transfers between devices, halving_psum(): other = lax.ppermute(cur, axis, [(i, i ^ bit) for i in range(count)])  21.2 us
    ppermute x3, starting transfers between devices, with_halo(): lax.ppermute(head, axis, [((i + 1) % count, i) for i in range(ends)])  8.76 us
    ppermute x3, starting transfers between devices, with_halo(): lax.ppermute(tail, axis, [(i, (i + 1) % count) for i in range(ends)])  7.63 us
    dot_general x1, matrix products, local(): jnp.einsum('koc,koiq->ciq', mixing, spread, preferred_element_type=jnp.fl...  7.27 us
    ppermute x5, starting transfers between devices, halving_psum(): other = lax.ppermute(cur, axis, [(i, i ^ bit) for i in range(count)])  6.21 us
  transfers between devices with their start and end apart: 16, of which 9 were waited for; matrix products, arithmetic and copies ran while one was open for 34% of the time, Pallas kernels for 0%

profile of v1, /device:TPU:0, one launch (start us, length us, event | category | flops | bytes accessed | tf_op | source)
XLA Modules:
  0.0 179.4 jit_solution(16364158500473745821)
XLA Ops:
  0.6 0.0 copy-start
  0.7 0.8 compare_convert_fusion
  1.5 0.8 broadcast_multiply_fusion.1
  2.3 1.3 collective-permute-start
  3.6 1.6 copy.7
  5.3 6.1 %collective-permute-start.2 = (bf16[256,8,16]{0,2,1:T(8,128)(2,1)S(1)}, bf16[256,8,16]{0,2,1:T(8,128)(2,1)S(1)}, u32[]{:S(2)}, u32[]{:S(2)}) collective-permute-start(bf16[256,8,16]{0,2,1:T(8,128)(2,1)S(1)} %get-tuple-element.9), channel_id=1, source_target_pairs={{4,0},{8,4},{12,8},{16,12},{20,16},{24,20},{28,24},{0,28},{5,1},{9... | collective-permute-start | bytes 196616 | tf_op jit(solution)/shard_map/ppermute | solution.py:22
  11.4 0.0 collective-permute-start.1
  11.4 2.7 %collective-permute-start.4 = (bf16[9,1,3,33]{3,1,2,0:T(2,128)(2,1)S(1)}, bf16[9,1,3,33]{3,1,2,0:T(2,128)(2,1)S(1)}, u32[]{:S(2)}, u32[]{:S(2)}) collective-permute-start(bf16[9,1,3,33]{3,1,2,0:T(2,128)(2,1)S(1)} %get-tuple-element.10), channel_id=1, source_target_pairs={{0,1},{1,2},{2,3},{4,5},{5,6},{6,7},{8,9},{9,10},{10,11},{12,13},{... | collective-permute-start | bytes 5354 | tf_op jit(solution)/shard_map/ppermute | solution.py:20
  14.1 1.3 fusion.3
  15.4 0.0 copy-start.1
  15.4 6.6 %fusion.7 = bf16[9,8,288,256]{3,1,2,0:T(8,128)(2,1)} fusion(pred[33,288,256,1]{2,1,0,3:T(32,128)(4,1)S(1)} %fusion.3, bf16[9,8,3,33]{3,1,2,0:T(8,128)(2,1)S(1)} %broadcast_multiply_fusion.1), kind=kOutput, calls=%fused_computation.12 | convolution fusion | flops 350355456 | bytes 13068288 | tf_op jit(solution)/shard_map/bpq,kib->kipq/dot_general | solution.py:73
  22.0 0.0 collective-permute-done
  22.0 8.6 %fusion.9 = bf16[9,8,288,256]{3,1,2,0:T(8,128)(2,1)} fusion(pred[33,288,256,1]{2,1,0,3:T(32,128)(4,1)} %copy-done.1, bf16[9,1,3,33]{3,1,2,0:T(2,128)(2,1)S(1)} %collective-permute-done, bf16[9,8,3,33]{3,1,2,0:T(8,128)(2,1)S(1)} %broadcast_multiply_fusion.1), kind=kOutput, calls=%fused_computation.14 | convolution fusion | flops 350364960 | bytes 13065894 | tf_op jit(solution)/shard_map/bpq,kib->kipq/dot_general | solution.py:73
  30.6 0.0 collective-permute-done.4
  30.6 6.6 %fusion.5 = bf16[9,8,288,256]{3,1,2,0:T(8,128)(2,1)} fusion(pred[33,288,256,1]{2,1,0,3:T(32,128)(4,1)S(1)} %copy-done.2, bf16[9,8,3,33]{3,1,2,0:T(8,128)(2,1)S(1)} %broadcast_multiply_fusion.1, bf16[9,1,3,33]{3,1,2,0:T(2,128)(2,1)S(1)} %collective-permute-done.4), kind=kOutput, calls=%fused_computation.10 | convolution fusion | flops 350364960 | bytes 13065894 | tf_op jit(solution)/shard_map/bpq,kib->kipq/dot_general | solution.py:73
  37.3 0.0 collective-permute-done.2
  37.3 0.0 collective-permute-done.1
  37.3 0.1 pad_maximum_fusion.10
  37.4 0.0 slice-start
  37.4 0.7 fusion.32
  38.1 1.4 collective-permute-start.3
  39.5 0.0 slice-start.1
  39.5 0.0 slice-start.2
  39.6 4.9 %collective-permute-start.5 = (bf16[256,1,288]{0,2,1:T(8,128)(2,1)}, bf16[256,1,288]{0,2,1:T(8,128)(2,1)}, u32[]{:S(2)}, u32[]{:S(2)}) collective-permute-start(bf16[256,1,288]{0,2,1:T(8,128)(2,1)} %get-tuple-element.6), channel_id=1, source_target_pairs={{0,1},{1,2},{2,3},{4,5},{5,6},{6,7},{8,9},{9,10},{10,11},{12,13},{... | collective-permute-start | bytes 442376 | tf_op jit(solution)/shard_map/ppermute | solution.py:20
  44.4 12.9 %fusion.1 = f32[8,9,256,256]{3,2,1,0:T(8,128)} fusion(bf16[9,8,288,256]{3,1,2,0:T(8,128)(2,1)} %fusion.7, bf16[256,8,16]{0,2,1:T(8,128)(2,1)S(1)} %collective-permute-done.2, bf16[256,8,256]{0,2,1:T(8,128)(2,1)S(1)} %copy.7, bf16[256,8,16]{0,2,1:T(8,128)(2,1)S(1)} %collective-permute-done.1), kind=kOutput, calls=%fused_computation.5 | convolution fusion | flops 2721447936 | bytes 30670848 | tf_op jit(solution)/shard_map/oip,kipq->koiq/dot_general | solution.py:76
  57.4 0.0 collective-permute-done.3
  57.4 0.0 slice-done.1
  57.4 12.4 %fusion = f32[8,9,256,256]{3,2,1,0:T(8,128)} fusion(bf16[9,8,288,256]{3,1,2,0:T(8,128)(2,1)S(1)} %bitcast.55, bf16[256,1,288]{0,2,1:T(8,128)(2,1)} %collective-permute-done.3, bf16[256,8,16]{0,2,1:T(8,128)(2,1)S(1)} %collective-permute-done.2, bf16[256,8,256]{0,2,1:T(8,128)(2,1)S(1)} %copy.7, bf16[256,8,16]{0,2,1:T(8,128)(2,1)S(1)} %collective-permute-done.1), kind=kOutput, calls=%fused_computation.4 | convolution fusion | flops 2722627584 | bytes 30818304 | tf_op jit(solution)/shard_map/oip,kipq->koiq/dot_general | solution.py:76
  69.8 0.0 collective-permute-done.5
  69.8 21.9 %fusion.4 = bf16[9,256,8,256]{1,3,0,2:T(8,128)(2,1)} fusion(f32[8,9,256,256]{3,2,1,0:T(8,128)} %fusion, f32[8,9,256,256]{3,2,1,0:T(8,128)} %fusion.1, bf16[9,8,288,256]{3,1,2,0:T(8,128)(2,1)} %fusion.5, bf16[256,1,288]{0,2,1:T(8,128)(2,1)} %collective-permute-done.5, bf16[256,8,16]{0,2,1:T(8,128)(2,1)S(1)} %collective-permute-done.2, ...), kind=kOutput, calls=%fused_computation.9 | convolution fusion | flops 2736783360 | bytes 59129856 | tf_op jit(solution)/shard_map/oip,kipq->koiq/dot_general | solution.py:76
  91.7 0.0 copy-done.4
  91.7 5.5 %fusion.20 = f32[9,256,256,1]{2,1,0,3:T(8,128)S(1)} fusion(bf16[9,256,8,256]{1,3,0,2:T(8,128)(2,1)} %fusion.4, bf16[256,8,256,1]{2,1,0,3:T(8,128)(2,1)S(1)} %bitcast.59), kind=kOutput, calls=%fused_computation.33 | convolution fusion | flops 2415919104 | bytes 12845056 | tf_op jit(solution)/shard_map/koiq,ciq->koc/dot_general | solution.py:94
  97.2 0.0 copy-start.3
  97.2 1.4 copy-done.3
  98.6 0.1 constant_dynamic-slice_fusion.4
  98.6 1.3 collective-permute-start.6
  100.0 2.5 %collective-permute-done.6 = f32[1152,256]{1,0:T(8,128)S(1)} collective-permute-done((f32[1152,256]{1,0:T(8,128)S(1)}, f32[1152,256]{1,0:T(8,128)S(1)}, u32[]{:S(2)}, u32[]{:S(2)}) %collective-permute-start.6) | collective-permute-done | bytes 1179680 | tf_op jit(solution)/shard_map/ppermute | solution.py:45
  102.5 1.4 dynamic-slice_add_fusion
  103.9 0.5 collective-permute-start.7
  104.4 15.2 %collective-permute-done.7 = f32[576,256]{1,0:T(8,128)S(1)} collective-permute-done((f32[576,256]{1,0:T(8,128)S(1)}, f32[576,256]{1,0:T(8,128)S(1)}, u32[]{:S(2)}, u32[]{:S(2)}) %collective-permute-start.7) | collective-permute-done | bytes 589856 | tf_op jit(solution)/shard_map/ppermute | solution.py:45
  119.6 0.1 dynamic-slice_add_fusion.1
  119.7 0.1 collective-permute-start.8
  119.8 8.4 %collective-permute-done.8 = f32[288,256]{1,0:T(8,128)S(1)} collective-permute-done((f32[288,256]{1,0:T(8,128)S(1)}, f32[288,256]{1,0:T(8,128)S(1)}, u32[]{:S(2)}, u32[]{:S(2)}) %collective-permute-start.8) | collective-permute-done | bytes 294944 | tf_op jit(solution)/shard_map/ppermute | solution.py:45
  128.3 0.1 collective-permute-start.9
  128.4 5.1 %collective-permute-done.9 = f32[144,256]{1,0:T(8,128)S(1)} collective-permute-done((f32[144,256]{1,0:T(8,128)S(1)}, f32[144,256]{1,0:T(8,128)S(1)}, u32[]{:S(2)}, u32[]{:S(2)}) %collective-permute-start.9) | collective-permute-done | bytes 147488 | tf_op jit(solution)/shard_map/ppermute | solution.py:45
  133.5 2.2 %collective-permute-start.10 = (f32[72,256]{1,0:T(8,128)S(1)}, f32[72,256]{1,0:T(8,128)S(1)}, u32[]{:S(2)}, u32[]{:S(2)}) collective-permute-start(f32[72,256]{1,0:T(8,128)S(1)} %constant_dynamic-slice_fusion), channel_id=1, source_target_pairs={{0,16},{4,20},{8,24},{12,28},{16,0},{20,4},{24,8},{28,12},{1,17},{... | collective-permute-start | bytes 221192 | tf_op jit(solution)/shard_map/ppermute | solution.py:45
  135.7 4.0 %collective-permute-done.10 = f32[72,256]{1,0:T(8,128)S(1)} collective-permute-done((f32[72,256]{1,0:T(8,128)S(1)}, f32[72,256]{1,0:T(8,128)S(1)}, u32[]{:S(2)}, u32[]{:S(2)}) %collective-permute-start.10) | collective-permute-done | bytes 73760 | tf_op jit(solution)/shard_map/ppermute | solution.py:45
  139.7 1.4 collective-permute-start.11
  141.1 4.1 %collective-permute-done.11 = f32[72,256]{1,0:T(8,128)S(1)} collective-permute-done((f32[72,256]{1,0:T(8,128)S(1)}, f32[72,256]{1,0:T(8,128)S(1)}, u32[]{:S(2)}, u32[]{:S(2)}) %collective-permute-start.11) | collective-permute-done | bytes 73760 | tf_op jit(solution)/shard_map/ppermute | solution.py:49
  145.2 2.3 %collective-permute-start.12 = (f32[144,256]{1,0:T(8,128)S(1)}, f32[144,256]{1,0:T(8,128)S(1)}, u32[]{:S(2)}, u32[]{:S(2)}) collective-permute-start(f32[144,256]{1,0:T(8,128)S(1)} %constant_dynamic-update-slice_fusion.8), channel_id=1, source_target_pairs={{0,8},{4,12},{8,0},{12,4},{16,24},{20,28},{24,16},{28,20},{1,9},{5... | collective-permute-start | bytes 442376 | tf_op jit(solution)/shard_map/ppermute | solution.py:49
  147.5 3.1 %collective-permute-done.12 = f32[144,256]{1,0:T(8,128)S(1)} collective-permute-done((f32[144,256]{1,0:T(8,128)S(1)}, f32[144,256]{1,0:T(8,128)S(1)}, u32[]{:S(2)}, u32[]{:S(2)}) %collective-permute-start.12) | collective-permute-done | bytes 147488 | tf_op jit(solution)/shard_map/ppermute | solution.py:49
  150.6 2.2 %collective-permute-start.13 = (f32[288,256]{1,0:T(8,128)S(1)}, f32[288,256]{1,0:T(8,128)S(1)}, u32[]{:S(2)}, u32[]{:S(2)}) collective-permute-start(f32[288,256]{1,0:T(8,128)S(1)} %constant_dynamic-update-slice_fusion.6), channel_id=1, source_target_pairs={{0,4},{4,0},{8,12},{12,8},{16,20},{20,16},{24,28},{28,24},{1,5},{5... | collective-permute-start | bytes 884744 | tf_op jit(solution)/shard_map/ppermute | solution.py:49
  152.8 4.6 %collective-permute-done.13 = f32[288,256]{1,0:T(8,128)S(1)} collective-permute-done((f32[288,256]{1,0:T(8,128)S(1)}, f32[288,256]{1,0:T(8,128)S(1)}, u32[]{:S(2)}, u32[]{:S(2)}) %collective-permute-start.13) | collective-permute-done | bytes 294944 | tf_op jit(solution)/shard_map/ppermute | solution.py:49
  157.5 0.3 collective-permute-start.14
  157.8 0.1 broadcast_in_dim.22
  158.0 9.5 %collective-permute-done.14 = f32[576,256]{1,0:T(8,128)S(1)} collective-permute-done((f32[576,256]{1,0:T(8,128)S(1)}, f32[576,256]{1,0:T(8,128)S(1)}, u32[]{:S(2)}, u32[]{:S(2)}) %collective-permute-start.14) | collective-permute-done | bytes 589856 | tf_op jit(solution)/shard_map/ppermute | solution.py:49
  167.5 0.1 collective-permute-start.15
  167.6 7.3 %fusion.11 = bf16[256,8,256]{0,2,1:T(8,128)(2,1)} fusion(bf16[9,256,8,256]{1,3,0,2:T(8,128)(2,1)} %fusion.4, bf16[9,256,256]{2,1,0:T(8,128)(2,1)S(1)} %copy-done), kind=kOutput, calls=%fused_computation.17 | convolution fusion | flops 2416443392 | bytes 11665408 | tf_op jit(solution)/shard_map/koc,koiq->ciq/dot_general | solution.py:97
  174.8 2.6 %copy.12 = bf16[256,8,256]{2,1,0:T(8,128)(2,1)} copy(bf16[256,8,256]{0,2,1:T(8,128)(2,1)} %fusion.11) | data formatting | bytes 2097152
  177.5 0.2 broadcast_in_dim.10
  177.6 0.1 constant_dynamic-update-slice_fusion.1
  177.7 0.0 collective-permute-done.15
  177.7 0.1 constant_dynamic-update-slice_fusion
  177.8 1.6 broadcast_multiply_fusion
  (30 shorter events, 0.5 us)
Async XLA Ops:
  0.6 166.9 %copy-start = (bf16[9,256,256]{2,1,0:T(8,128)(2,1)S(1)}, bf16[9,256,256]{2,1,0:T(8,128)(2,1)}, u32[]{:S(2)}) copy-start(bf16[9,256,256]{2,1,0:T(8,128)(2,1)} %param.7) | copy-start | bytes 3538948
  2.3 19.7 %collective-permute-start = (bf16[9,1,3,33]{3,1,2,0:T(2,128)(2,1)S(1)}, bf16[9,1,3,33]{3,1,2,0:T(2,128)(2,1)S(1)}, u32[]{:S(2)}, u32[]{:S(2)}) collective-permute-start(bf16[9,1,3,33]{3,1,2,0:T(2,128)(2,1)S(1)} %get-tuple-element.11), channel_id=1, source_target_pairs={{1,0},{2,1},{3,2},{5,4},{6,5},{7,6},{9,8},{10,9},{11,10},{13,12},{... | collective-permute-start | bytes 5354 | tf_op jit(solution)/shard_map/ppermute | solution.py:22
  5.3 32.0 %collective-permute-start.2 = (bf16[256,8,16]{0,2,1:T(8,128)(2,1)S(1)}, bf16[256,8,16]{0,2,1:T(8,128)(2,1)S(1)}, u32[]{:S(2)}, u32[]{:S(2)}) collective-permute-start(bf16[256,8,16]{0,2,1:T(8,128)(2,1)S(1)} %get-tuple-element.9), channel_id=1, source_target_pairs={{4,0},{8,4},{12,8},{16,12},{20,16},{24,20},{28,24},{0,28},{5,1},{9... | collective-permute-start | bytes 196616 | tf_op jit(solution)/shard_map/ppermute | solution.py:22
  11.4 25.9 %collective-permute-start.1 = (bf16[256,8,16]{0,2,1:T(8,128)(2,1)S(1)}, bf16[256,8,16]{0,2,1:T(8,128)(2,1)S(1)}, u32[]{:S(2)}, u32[]{:S(2)}) collective-permute-start(bf16[256,8,16]{0,2,1:T(8,128)(2,1)S(1)} %get-tuple-element.8), channel_id=1, source_target_pairs={{0,4},{4,8},{8,12},{12,16},{16,20},{20,24},{24,28},{28,0},{1,5},{5... | collective-permute-start | bytes 196616 | tf_op jit(solution)/shard_map/ppermute | solution.py:20
  11.4 19.3 %collective-permute-start.4 = (bf16[9,1,3,33]{3,1,2,0:T(2,128)(2,1)S(1)}, bf16[9,1,3,33]{3,1,2,0:T(2,128)(2,1)S(1)}, u32[]{:S(2)}, u32[]{:S(2)}) collective-permute-start(bf16[9,1,3,33]{3,1,2,0:T(2,128)(2,1)S(1)} %get-tuple-element.10), channel_id=1, source_target_pairs={{0,1},{1,2},{2,3},{4,5},{5,6},{6,7},{8,9},{9,10},{10,11},{12,13},{... | collective-permute-start | bytes 5354 | tf_op jit(solution)/shard_map/ppermute | solution.py:20
  15.4 6.6 %copy-start.1 = (pred[33,288,256,1]{2,1,0,3:T(32,128)(4,1)}, pred[33,288,256,1]{2,1,0,3:T(32,128)(4,1)S(1)}, u32[]{:S(2)}) copy-start(pred[33,288,256,1]{2,1,0,3:T(32,128)(4,1)S(1)} %fusion.3) | copy-start | bytes 7299076
  22.0 8.6 %copy-start.2 = (pred[33,288,256,1]{2,1,0,3:T(32,128)(4,1)S(1)}, pred[33,288,256,1]{2,1,0,3:T(32,128)(4,1)}, u32[]{:S(2)}) copy-start(pred[33,288,256,1]{2,1,0,3:T(32,128)(4,1)} %copy-done.1) | copy-start | bytes 7299076
  37.4 20.0 %slice-start = ((s8[10616832]{0:T(1024)(128)(4,1)}), s8[4194304]{0:T(1024)(128)(4,1)S(1)}, s32[]{:S(2)}) async-start(s8[10616832]{0:T(1024)(128)(4,1)} %bitcast.54), calls=%async_computation | async-start | bytes 8388608
  38.1 19.2 %collective-permute-start.3 = (bf16[256,1,288]{0,2,1:T(8,128)(2,1)}, bf16[256,1,288]{0,2,1:T(8,128)(2,1)}, u32[]{:S(2)}, u32[]{:S(2)}) collective-permute-start(bf16[256,1,288]{0,2,1:T(8,128)(2,1)} %get-tuple-element.7), channel_id=1, source_target_pairs={{1,0},{2,1},{3,2},{5,4},{6,5},{7,6},{9,8},{10,9},{11,10},{13,12},{... | collective-permute-start | bytes 442376 | tf_op jit(solution)/shard_map/ppermute | solution.py:22
  39.5 17.8 %slice-start.1 = ((s8[10616832]{0:T(1024)(128)(4,1)}), s8[4194304]{0:T(1024)(128)(4,1)S(1)}, s32[]{:S(2)}) async-start(s8[10616832]{0:T(1024)(128)(4,1)} %bitcast.54), calls=%async_computation.1 | async-start | bytes 8388608
  39.5 17.8 %slice-start.2 = ((s8[10616832]{0:T(1024)(128)(4,1)}), s8[2228224]{0:T(1024)(128)(4,1)S(1)}, s32[]{:S(2)}) async-start(s8[10616832]{0:T(1024)(128)(4,1)} %bitcast.54), calls=%async_computation.2 | async-start | bytes 4456448
  39.6 30.3 %collective-permute-start.5 = (bf16[256,1,288]{0,2,1:T(8,128)(2,1)}, bf16[256,1,288]{0,2,1:T(8,128)(2,1)}, u32[]{:S(2)}, u32[]{:S(2)}) collective-permute-start(bf16[256,1,288]{0,2,1:T(8,128)(2,1)} %get-tuple-element.6), channel_id=1, source_target_pairs={{0,1},{1,2},{2,3},{4,5},{5,6},{6,7},{8,9},{9,10},{10,11},{12,13},{... | collective-permute-start | bytes 442376 | tf_op jit(solution)/shard_map/ppermute | solution.py:20
  69.8 21.9 %copy-start.4 = (bf16[256,8,256]{2,1,0:T(8,128)(2,1)S(1)}, bf16[256,8,256]{2,1,0:T(8,128)(2,1)}, u32[]{:S(2)}) copy-start(bf16[256,8,256]{2,1,0:T(8,128)(2,1)} %param.5) | copy-start | bytes 3145732
  97.2 1.4 copy-start.3
  98.6 3.8 %collective-permute-start.6 = (f32[1152,256]{1,0:T(8,128)S(1)}, f32[1152,256]{1,0:T(8,128)S(1)}, u32[]{:S(2)}, u32[]{:S(2)}) collective-permute-start(f32[1152,256]{1,0:T(8,128)S(1)} %constant_dynamic-slice_fusion.4), channel_id=1, source_target_pairs={{0,1},{1,0},{2,3},{3,2},{4,5},{5,4},{6,7},{7,6},{8,9},{9,8},{10,11... | collective-permute-start | bytes 3538952 | tf_op jit(solution)/shard_map/ppermute | solution.py:45
  103.9 15.7 %collective-permute-start.7 = (f32[576,256]{1,0:T(8,128)S(1)}, f32[576,256]{1,0:T(8,128)S(1)}, u32[]{:S(2)}, u32[]{:S(2)}) collective-permute-start(f32[576,256]{1,0:T(8,128)S(1)} %constant_dynamic-slice_fusion.3), channel_id=1, source_target_pairs={{0,2},{1,3},{2,0},{3,1},{4,6},{5,7},{6,4},{7,5},{8,10},{9,11},{10,... | collective-permute-start | bytes 1769480 | tf_op jit(solution)/shard_map/ppermute | solution.py:45
  119.7 8.5 %collective-permute-start.8 = (f32[288,256]{1,0:T(8,128)S(1)}, f32[288,256]{1,0:T(8,128)S(1)}, u32[]{:S(2)}, u32[]{:S(2)}) collective-permute-start(f32[288,256]{1,0:T(8,128)S(1)} %constant_dynamic-slice_fusion.2), channel_id=1, source_target_pairs={{0,4},{4,0},{8,12},{12,8},{16,20},{20,16},{24,28},{28,24},{1,5},{5... | collective-permute-start | bytes 884744 | tf_op jit(solution)/shard_map/ppermute | solution.py:45
  128.3 5.2 %collective-permute-start.9 = (f32[144,256]{1,0:T(8,128)S(1)}, f32[144,256]{1,0:T(8,128)S(1)}, u32[]{:S(2)}, u32[]{:S(2)}) collective-permute-start(f32[144,256]{1,0:T(8,128)S(1)} %constant_dynamic-slice_fusion.1), channel_id=1, source_target_pairs={{0,8},{4,12},{8,0},{12,4},{16,24},{20,28},{24,16},{28,20},{1,9},{5... | collective-permute-start | bytes 442376 | tf_op jit(solution)/shard_map/ppermute | solution.py:45
  133.5 6.2 %collective-permute-start.10 = (f32[72,256]{1,0:T(8,128)S(1)}, f32[72,256]{1,0:T(8,128)S(1)}, u32[]{:S(2)}, u32[]{:S(2)}) collective-permute-start(f32[72,256]{1,0:T(8,128)S(1)} %constant_dynamic-slice_fusion), channel_id=1, source_target_pairs={{0,16},{4,20},{8,24},{12,28},{16,0},{20,4},{24,8},{28,12},{1,17},{... | collective-permute-start | bytes 221192 | tf_op jit(solution)/shard_map/ppermute | solution.py:45
  139.7 5.4 %collective-permute-start.11 = (f32[72,256]{1,0:T(8,128)S(1)}, f32[72,256]{1,0:T(8,128)S(1)}, u32[]{:S(2)}, u32[]{:S(2)}) collective-permute-start(f32[72,256]{1,0:T(8,128)S(1)} %get-tuple-element.5), channel_id=1, source_target_pairs={{0,16},{4,20},{8,24},{12,28},{16,0},{20,4},{24,8},{28,12},{1,17},{... | collective-permute-start | bytes 221192 | tf_op jit(solution)/shard_map/ppermute | solution.py:49
  145.2 5.4 %collective-permute-start.12 = (f32[144,256]{1,0:T(8,128)S(1)}, f32[144,256]{1,0:T(8,128)S(1)}, u32[]{:S(2)}, u32[]{:S(2)}) collective-permute-start(f32[144,256]{1,0:T(8,128)S(1)} %constant_dynamic-update-slice_fusion.8), channel_id=1, source_target_pairs={{0,8},{4,12},{8,0},{12,4},{16,24},{20,28},{24,16},{28,20},{1,9},{5... | collective-permute-start | bytes 442376 | tf_op jit(solution)/shard_map/ppermute | solution.py:49
  150.6 6.9 %collective-permute-start.13 = (f32[288,256]{1,0:T(8,128)S(1)}, f32[288,256]{1,0:T(8,128)S(1)}, u32[]{:S(2)}, u32[]{:S(2)}) collective-permute-start(f32[288,256]{1,0:T(8,128)S(1)} %constant_dynamic-update-slice_fusion.6), channel_id=1, source_target_pairs={{0,4},{4,0},{8,12},{12,8},{16,20},{20,16},{24,28},{28,24},{1,5},{5... | collective-permute-start | bytes 884744 | tf_op jit(solution)/shard_map/ppermute | solution.py:49
  157.5 9.9 %collective-permute-start.14 = (f32[576,256]{1,0:T(8,128)S(1)}, f32[576,256]{1,0:T(8,128)S(1)}, u32[]{:S(2)}, u32[]{:S(2)}) collective-permute-start(f32[576,256]{1,0:T(8,128)S(1)} %constant_dynamic-update-slice_fusion.4), channel_id=1, source_target_pairs={{0,2},{1,3},{2,0},{3,1},{4,6},{5,7},{6,4},{7,5},{8,10},{9,11},{10,... | collective-permute-start | bytes 1769480 | tf_op jit(solution)/shard_map/ppermute | solution.py:49
  167.5 10.3 %collective-permute-start.15 = (f32[1152,256]{1,0:T(8,128)S(1)}, f32[1152,256]{1,0:T(8,128)S(1)}, u32[]{:S(2)}, u32[]{:S(2)}) collective-permute-start(f32[1152,256]{1,0:T(8,128)S(1)} %constant_dynamic-update-slice_fusion.2), channel_id=1, source_target_pairs={{0,1},{1,0},{2,3},{3,2},{4,5},{5,4},{6,7},{7,6},{8,9},{9,8},{10,11... | collective-permute-start | bytes 3538952 | tf_op jit(solution)/shard_map/ppermute | solution.py:49

commit v2 on v1

--- a/solution.py
+++ b/solution.py
@@ -42,7 +42,8 @@
         half = cur.shape[0] // 2
         keep = lax.dynamic_slice_in_dim(cur, side * half, half, 0)
         send = lax.dynamic_slice_in_dim(cur, (1 - side) * half, half, 0)
-        cur = keep + lax.ppermute(send, axis, [(i, i ^ bit) for i in range(count)])
+        sent = lax.ppermute(send.astype(jnp.bfloat16), axis, [(i, i ^ bit) for i in range(count)])
+        cur = keep + sent.astype(cur.dtype)
     for axis, bit in reversed(stages):
         count = lax.axis_size(axis)
         side = (lax.axis_index(axis) // bit) % 2

time: 180 us -> 168 us (0.933)
  waiting for transfers between devices: 56.4 us -> 43.8 us
    ppermute x5, waiting for transfers between devices: 35.1 us -> 22.8 us  [halving_psum(): lax.ppermute(send.astype(jnp.bfloat16), axis, [(i, i ^ bit) for i in rang...]
  transfers between devices with their start and end apart: 16 -> 16, of which waited for: 9 -> 9; matrix products, arithmetic and copies ran while one was open for 34% -> 36% of each run, Pallas kernels for 0% -> 0%
where the time goes in v2:
time: 168 us; the launch traced here: 167 us
  matrix products  81.8 us (49%)
  waiting for transfers between devices  43.8 us (26%)
  starting transfers between devices  27.3 us (16%)
  local copies, waits for them, and re-layouts  7.27 us (4%)
  other arithmetic  6.09 us (4%)
    dot_general x3, matrix products, spread_block(): jnp.einsum('oip,kipq->koiq', rows_in, tiles, preferred_element_type=jnp.f...  47.2 us
    ppermute x5, waiting for transfers between devices, halving_psum(): lax.ppermute(send.astype(jnp.bfloat16), axis, [(i, i ^ bit) for i in rang...  22.8 us
    dot_general x3, matrix products, spread_block(): jnp.einsum('bpq,kib->kipq', selector, part_coefs, preferred_element_type=...  21.8 us
    ppermute x5, waiting for transfers between devices, halving_psum(): other = lax.ppermute(cur, axis, [(i, i ^ bit) for i in range(count)])  21 us
    ppermute x3, starting transfers between devices, with_halo(): lax.ppermute(head, axis, [((i + 1) % count, i) for i in range(ends)])  8.76 us
    ppermute x3, starting transfers between devices, with_halo(): lax.ppermute(tail, axis, [(i, (i + 1) % count) for i in range(ends)])  7.63 us
    dot_general x1, matrix products, local(): jnp.einsum('koc,koiq->ciq', mixing, spread, preferred_element_type=jnp.fl...  7.27 us
    ppermute x5, starting transfers between devices, halving_psum(): other = lax.ppermute(cur, axis, [(i, i ^ bit) for i in range(count)])  6.78 us
  transfers between devices with their start and end apart: 16, of which 9 were waited for; matrix products, arithmetic and copies ran while one was open for 36% of the time, Pallas kernels for 0%

profile of v2, /device:TPU:0, one launch (start us, length us, event | category | flops | bytes accessed | tf_op | source)
XLA Modules:
  0.0 167.3 jit_solution(13702623960062781149)
XLA Ops:
  0.6 0.0 copy-start
  0.7 0.8 compare_convert_fusion
  1.5 0.8 broadcast_multiply_fusion.1
  2.3 1.3 collective-permute-start
  3.6 1.6 copy.7
  5.3 6.1 %collective-permute-start.2 = (bf16[256,8,16]{0,2,1:T(8,128)(2,1)S(1)}, bf16[256,8,16]{0,2,1:T(8,128)(2,1)S(1)}, u32[]{:S(2)}, u32[]{:S(2)}) collective-permute-start(bf16[256,8,16]{0,2,1:T(8,128)(2,1)S(1)} %get-tuple-element.9), channel_id=1, source_target_pairs={{4,0},{8,4},{12,8},{16,12},{20,16},{24,20},{28,24},{0,28},{5,1},{9... | collective-permute-start | bytes 196616 | tf_op jit(solution)/shard_map/ppermute | solution.py:22
  11.4 0.0 collective-permute-start.1
  11.4 2.7 %collective-permute-start.4 = (bf16[9,1,3,33]{3,1,2,0:T(2,128)(2,1)S(1)}, bf16[9,1,3,33]{3,1,2,0:T(2,128)(2,1)S(1)}, u32[]{:S(2)}, u32[]{:S(2)}) collective-permute-start(bf16[9,1,3,33]{3,1,2,0:T(2,128)(2,1)S(1)} %get-tuple-element.10), channel_id=1, source_target_pairs={{0,1},{1,2},{2,3},{4,5},{5,6},{6,7},{8,9},{9,10},{10,11},{12,13},{... | collective-permute-start | bytes 5354 | tf_op jit(solution)/shard_map/ppermute | solution.py:20
  14.1 1.3 fusion.3
  15.4 6.6 %fusion.7 = bf16[9,8,288,256]{3,1,2,0:T(8,128)(2,1)} fusion(pred[33,288,256,1]{2,1,0,3:T(32,128)(4,1)S(1)} %fusion.3, bf16[9,8,3,33]{3,1,2,0:T(8,128)(2,1)S(1)} %broadcast_multiply_fusion.1), kind=kOutput, calls=%fused_computation.12 | convolution fusion | flops 350355456 | bytes 13068288 | tf_op jit(solution)/shard_map/bpq,kib->kipq/dot_general | solution.py:74
  22.0 0.0 copy-done.1
  22.0 0.0 collective-permute-done
  22.0 8.6 %fusion.9 = bf16[9,8,288,256]{3,1,2,0:T(8,128)(2,1)} fusion(pred[33,288,256,1]{2,1,0,3:T(32,128)(4,1)} %copy-done.1, bf16[9,1,3,33]{3,1,2,0:T(2,128)(2,1)S(1)} %collective-permute-done, bf16[9,8,3,33]{3,1,2,0:T(8,128)(2,1)S(1)} %broadcast_multiply_fusion.1), kind=kOutput, calls=%fused_computation.14 | convolution fusion | flops 350364960 | bytes 13065894 | tf_op jit(solution)/shard_map/bpq,kib->kipq/dot_general | solution.py:74
  30.6 0.0 collective-permute-done.4
  30.6 0.0 copy-done.2
  30.6 6.6 %fusion.5 = bf16[9,8,288,256]{3,1,2,0:T(8,128)(2,1)} fusion(pred[33,288,256,1]{2,1,0,3:T(32,128)(4,1)S(1)} %copy-done.2, bf16[9,8,3,33]{3,1,2,0:T(8,128)(2,1)S(1)} %broadcast_multiply_fusion.1, bf16[9,1,3,33]{3,1,2,0:T(2,128)(2,1)S(1)} %collective-permute-done.4), kind=kOutput, calls=%fused_computation.10 | convolution fusion | flops 350364960 | bytes 13065894 | tf_op jit(solution)/shard_map/bpq,kib->kipq/dot_general | solution.py:74
  37.3 0.0 collective-permute-done.2
  37.3 0.0 collective-permute-done.1
  37.3 0.1 pad_maximum_fusion.10
  37.4 0.0 slice-start
  37.4 0.7 fusion.32
  38.1 1.4 collective-permute-start.3
  39.5 0.0 slice-start.1
  39.5 0.0 slice-start.2
  39.6 4.9 %collective-permute-start.5 = (bf16[256,1,288]{0,2,1:T(8,128)(2,1)}, bf16[256,1,288]{0,2,1:T(8,128)(2,1)}, u32[]{:S(2)}, u32[]{:S(2)}) collective-permute-start(bf16[256,1,288]{0,2,1:T(8,128)(2,1)} %get-tuple-element.6), channel_id=1, source_target_pairs={{0,1},{1,2},{2,3},{4,5},{5,6},{6,7},{8,9},{9,10},{10,11},{12,13},{... | collective-permute-start | bytes 442376 | tf_op jit(solution)/shard_map/ppermute | solution.py:20
  44.4 12.9 %fusion.1 = f32[8,9,256,256]{3,2,1,0:T(8,128)} fusion(bf16[9,8,288,256]{3,1,2,0:T(8,128)(2,1)} %fusion.7, bf16[256,8,16]{0,2,1:T(8,128)(2,1)S(1)} %collective-permute-done.2, bf16[256,8,256]{0,2,1:T(8,128)(2,1)S(1)} %copy.7, bf16[256,8,16]{0,2,1:T(8,128)(2,1)S(1)} %collective-permute-done.1), kind=kOutput, calls=%fused_computation.5 | convolution fusion | flops 2721447936 | bytes 30670848 | tf_op jit(solution)/shard_map/oip,kipq->koiq/dot_general | solution.py:77
  57.4 0.0 collective-permute-done.3
  57.4 0.0 slice-done
  57.4 12.4 %fusion = f32[8,9,256,256]{3,2,1,0:T(8,128)} fusion(bf16[9,8,288,256]{3,1,2,0:T(8,128)(2,1)S(1)} %bitcast.55, bf16[256,1,288]{0,2,1:T(8,128)(2,1)} %collective-permute-done.3, bf16[256,8,16]{0,2,1:T(8,128)(2,1)S(1)} %collective-permute-done.2, bf16[256,8,256]{0,2,1:T(8,128)(2,1)S(1)} %copy.7, bf16[256,8,16]{0,2,1:T(8,128)(2,1)S(1)} %collective-permute-done.1), kind=kOutput, calls=%fused_computation.4 | convolution fusion | flops 2722627584 | bytes 30818304 | tf_op jit(solution)/shard_map/oip,kipq->koiq/dot_general | solution.py:77
  69.8 0.0 collective-permute-done.5
  69.8 21.9 %fusion.4 = bf16[9,256,8,256]{1,3,0,2:T(8,128)(2,1)} fusion(f32[8,9,256,256]{3,2,1,0:T(8,128)} %fusion, f32[8,9,256,256]{3,2,1,0:T(8,128)} %fusion.1, bf16[9,8,288,256]{3,1,2,0:T(8,128)(2,1)} %fusion.5, bf16[256,1,288]{0,2,1:T(8,128)(2,1)} %collective-permute-done.5, bf16[256,8,16]{0,2,1:T(8,128)(2,1)S(1)} %collective-permute-done.2, ...), kind=kOutput, calls=%fused_computation.9 | convolution fusion | flops 2736783360 | bytes 59129856 | tf_op jit(solution)/shard_map/oip,kipq->koiq/dot_general | solution.py:77
  91.7 5.5 %fusion.20 = f32[9,256,256,1]{2,1,0,3:T(8,128)S(1)} fusion(bf16[9,256,8,256]{1,3,0,2:T(8,128)(2,1)} %fusion.4, bf16[256,8,256,1]{2,1,0,3:T(8,128)(2,1)S(1)} %bitcast.59), kind=kOutput, calls=%fused_computation.34 | convolution fusion | flops 2415919104 | bytes 12845056 | tf_op jit(solution)/shard_map/koiq,ciq->koc/dot_general | solution.py:95
  97.2 0.0 copy-start.3
  97.2 1.4 copy-done.3
  98.6 0.1 dynamic-slice_convert_fusion
  98.6 1.3 collective-permute-start.6
  100.0 1.6 collective-permute-done.6
  101.6 1.4 convert_add_fusion
  103.0 0.5 collective-permute-start.7
  103.5 8.9 %collective-permute-done.7 = bf16[576,256]{1,0:T(8,128)(2,1)S(1)} collective-permute-done((bf16[576,256]{1,0:T(8,128)(2,1)S(1)}, bf16[576,256]{1,0:T(8,128)(2,1)S(1)}, u32[]{:S(2)}, u32[]{:S(2)}) %collective-permute-start.7) | collective-permute-done | bytes 294944 | tf_op jit(solution)/shard_map/ppermute | solution.py:45
  112.4 0.1 convert_add_fusion.1
  112.5 0.1 collective-permute-start.8
  112.6 5.2 %collective-permute-done.8 = bf16[288,256]{1,0:T(8,128)(2,1)S(1)} collective-permute-done((bf16[288,256]{1,0:T(8,128)(2,1)S(1)}, bf16[288,256]{1,0:T(8,128)(2,1)S(1)}, u32[]{:S(2)}, u32[]{:S(2)}) %collective-permute-start.8) | collective-permute-done | bytes 147488 | tf_op jit(solution)/shard_map/ppermute | solution.py:45
  117.9 0.1 collective-permute-start.9
  118.0 4.3 %collective-permute-done.9 = bf16[144,256]{1,0:T(8,128)(2,1)S(1)} collective-permute-done((bf16[144,256]{1,0:T(8,128)(2,1)S(1)}, bf16[144,256]{1,0:T(8,128)(2,1)S(1)}, u32[]{:S(2)}, u32[]{:S(2)}) %collective-permute-start.9) | collective-permute-done | bytes 73760 | tf_op jit(solution)/shard_map/ppermute | solution.py:45
  122.3 2.2 %collective-permute-start.10 = (bf16[72,256]{1,0:T(8,128)(2,1)S(1)}, bf16[72,256]{1,0:T(8,128)(2,1)S(1)}, u32[]{:S(2)}, u32[]{:S(2)}) collective-permute-start(bf16[72,256]{1,0:T(8,128)(2,1)S(1)} %dynamic-slice_convert_fusion.4), channel_id=1, source_target_pairs={{0,16},{4,20},{8,24},{12,28},{16,0},{20,4},{24,8},{28,12},{1,17},{... | collective-permute-start | bytes 110600 | tf_op jit(solution)/shard_map/ppermute | solution.py:45
  124.5 2.8 %collective-permute-done.10 = bf16[72,256]{1,0:T(8,128)(2,1)S(1)} collective-permute-done((bf16[72,256]{1,0:T(8,128)(2,1)S(1)}, bf16[72,256]{1,0:T(8,128)(2,1)S(1)}, u32[]{:S(2)}, u32[]{:S(2)}) %collective-permute-start.10) | collective-permute-done | bytes 36896 | tf_op jit(solution)/shard_map/ppermute | solution.py:45
  127.3 2.2 %collective-permute-start.11 = (f32[72,256]{1,0:T(8,128)S(1)}, f32[72,256]{1,0:T(8,128)S(1)}, u32[]{:S(2)}, u32[]{:S(2)}) collective-permute-start(f32[72,256]{1,0:T(8,128)S(1)} %get-tuple-element.5), channel_id=1, source_target_pairs={{0,16},{4,20},{8,24},{12,28},{16,0},{20,4},{24,8},{28,12},{1,17},{... | collective-permute-start | bytes 221192 | tf_op jit(solution)/shard_map/ppermute | solution.py:50
  129.5 3.2 %collective-permute-done.11 = f32[72,256]{1,0:T(8,128)S(1)} collective-permute-done((f32[72,256]{1,0:T(8,128)S(1)}, f32[72,256]{1,0:T(8,128)S(1)}, u32[]{:S(2)}, u32[]{:S(2)}) %collective-permute-start.11) | collective-permute-done | bytes 73760 | tf_op jit(solution)/shard_map/ppermute | solution.py:50
  132.7 1.5 collective-permute-start.12
  134.3 3.7 %collective-permute-done.12 = f32[144,256]{1,0:T(8,128)S(1)} collective-permute-done((f32[144,256]{1,0:T(8,128)S(1)}, f32[144,256]{1,0:T(8,128)S(1)}, u32[]{:S(2)}, u32[]{:S(2)}) %collective-permute-start.12) | collective-permute-done | bytes 147488 | tf_op jit(solution)/shard_map/ppermute | solution.py:50
  138.0 2.7 %collective-permute-start.13 = (f32[288,256]{1,0:T(8,128)S(1)}, f32[288,256]{1,0:T(8,128)S(1)}, u32[]{:S(2)}, u32[]{:S(2)}) collective-permute-start(f32[288,256]{1,0:T(8,128)S(1)} %constant_dynamic-update-slice_fusion.6), channel_id=1, source_target_pairs={{0,4},{4,0},{8,12},{12,8},{16,20},{20,16},{24,28},{28,24},{1,5},{5... | collective-permute-start | bytes 884744 | tf_op jit(solution)/shard_map/ppermute | solution.py:50
  140.7 4.6 %collective-permute-done.13 = f32[288,256]{1,0:T(8,128)S(1)} collective-permute-done((f32[288,256]{1,0:T(8,128)S(1)}, f32[288,256]{1,0:T(8,128)S(1)}, u32[]{:S(2)}, u32[]{:S(2)}) %collective-permute-start.13) | collective-permute-done | bytes 294944 | tf_op jit(solution)/shard_map/ppermute | solution.py:50
  145.4 0.4 collective-permute-start.14
  145.7 0.1 broadcast_in_dim.22
  145.9 9.4 %collective-permute-done.14 = f32[576,256]{1,0:T(8,128)S(1)} collective-permute-done((f32[576,256]{1,0:T(8,128)S(1)}, f32[576,256]{1,0:T(8,128)S(1)}, u32[]{:S(2)}, u32[]{:S(2)}) %collective-permute-start.14) | collective-permute-done | bytes 589856 | tf_op jit(solution)/shard_map/ppermute | solution.py:50
  155.4 0.1 collective-permute-start.15
  155.4 7.3 %fusion.11 = bf16[256,8,256]{0,2,1:T(8,128)(2,1)} fusion(bf16[9,256,8,256]{1,3,0,2:T(8,128)(2,1)} %fusion.4, bf16[9,256,256]{2,1,0:T(8,128)(2,1)S(1)} %copy-done), kind=kOutput, calls=%fused_computation.17 | convolution fusion | flops 2416443392 | bytes 11665408 | tf_op jit(solution)/shard_map/koc,koiq->ciq/dot_general | solution.py:98
  162.7 2.6 %copy.12 = bf16[256,8,256]{2,1,0:T(8,128)(2,1)} copy(bf16[256,8,256]{0,2,1:T(8,128)(2,1)} %fusion.11) | data formatting | bytes 2097152
  165.4 0.2 broadcast_in_dim.10
  165.5 0.1 constant_dynamic-update-slice_fusion.1
  165.6 0.0 collective-permute-done.15
  165.6 0.1 constant_dynamic-update-slice_fusion
  165.7 1.6 broadcast_multiply_fusion
  (30 shorter events, 0.5 us)
Async XLA Ops:
  0.6 154.8 %copy-start = (bf16[9,256,256]{2,1,0:T(8,128)(2,1)S(1)}, bf16[9,256,256]{2,1,0:T(8,128)(2,1)}, u32[]{:S(2)}) copy-start(bf16[9,256,256]{2,1,0:T(8,128)(2,1)} %param.7) | copy-start | bytes 3538948
  2.3 19.7 %collective-permute-start = (bf16[9,1,3,33]{3,1,2,0:T(2,128)(2,1)S(1)}, bf16[9,1,3,33]{3,1,2,0:T(2,128)(2,1)S(1)}, u32[]{:S(2)}, u32[]{:S(2)}) collective-permute-start(bf16[9,1,3,33]{3,1,2,0:T(2,128)(2,1)S(1)} %get-tuple-element.11), channel_id=1, source_target_pairs={{1,0},{2,1},{3,2},{5,4},{6,5},{7,6},{9,8},{10,9},{11,10},{13,12},{... | collective-permute-start | bytes 5354 | tf_op jit(solution)/shard_map/ppermute | solution.py:22
  5.3 32.0 %collective-permute-start.2 = (bf16[256,8,16]{0,2,1:T(8,128)(2,1)S(1)}, bf16[256,8,16]{0,2,1:T(8,128)(2,1)S(1)}, u32[]{:S(2)}, u32[]{:S(2)}) collective-permute-start(bf16[256,8,16]{0,2,1:T(8,128)(2,1)S(1)} %get-tuple-element.9), channel_id=1, source_target_pairs={{4,0},{8,4},{12,8},{16,12},{20,16},{24,20},{28,24},{0,28},{5,1},{9... | collective-permute-start | bytes 196616 | tf_op jit(solution)/shard_map/ppermute | solution.py:22
  11.4 25.9 %collective-permute-start.1 = (bf16[256,8,16]{0,2,1:T(8,128)(2,1)S(1)}, bf16[256,8,16]{0,2,1:T(8,128)(2,1)S(1)}, u32[]{:S(2)}, u32[]{:S(2)}) collective-permute-start(bf16[256,8,16]{0,2,1:T(8,128)(2,1)S(1)} %get-tuple-element.8), channel_id=1, source_target_pairs={{0,4},{4,8},{8,12},{12,16},{16,20},{20,24},{24,28},{28,0},{1,5},{5... | collective-permute-start | bytes 196616 | tf_op jit(solution)/shard_map/ppermute | solution.py:20
  11.4 19.3 %collective-permute-start.4 = (bf16[9,1,3,33]{3,1,2,0:T(2,128)(2,1)S(1)}, bf16[9,1,3,33]{3,1,2,0:T(2,128)(2,1)S(1)}, u32[]{:S(2)}, u32[]{:S(2)}) collective-permute-start(bf16[9,1,3,33]{3,1,2,0:T(2,128)(2,1)S(1)} %get-tuple-element.10), channel_id=1, source_target_pairs={{0,1},{1,2},{2,3},{4,5},{5,6},{6,7},{8,9},{9,10},{10,11},{12,13},{... | collective-permute-start | bytes 5354 | tf_op jit(solution)/shard_map/ppermute | solution.py:20
  15.4 6.6 %copy-start.1 = (pred[33,288,256,1]{2,1,0,3:T(32,128)(4,1)}, pred[33,288,256,1]{2,1,0,3:T(32,128)(4,1)S(1)}, u32[]{:S(2)}) copy-start(pred[33,288,256,1]{2,1,0,3:T(32,128)(4,1)S(1)} %fusion.3) | copy-start | bytes 7299076
  22.0 8.6 %copy-start.2 = (pred[33,288,256,1]{2,1,0,3:T(32,128)(4,1)S(1)}, pred[33,288,256,1]{2,1,0,3:T(32,128)(4,1)}, u32[]{:S(2)}) copy-start(pred[33,288,256,1]{2,1,0,3:T(32,128)(4,1)} %copy-done.1) | copy-start | bytes 7299076
  37.4 20.0 %slice-start = ((s8[10616832]{0:T(1024)(128)(4,1)}), s8[4194304]{0:T(1024)(128)(4,1)S(1)}, s32[]{:S(2)}) async-start(s8[10616832]{0:T(1024)(128)(4,1)} %bitcast.54), calls=%async_computation | async-start | bytes 8388608
  38.1 19.2 %collective-permute-start.3 = (bf16[256,1,288]{0,2,1:T(8,128)(2,1)}, bf16[256,1,288]{0,2,1:T(8,128)(2,1)}, u32[]{:S(2)}, u32[]{:S(2)}) collective-permute-start(bf16[256,1,288]{0,2,1:T(8,128)(2,1)} %get-tuple-element.7), channel_id=1, source_target_pairs={{1,0},{2,1},{3,2},{5,4},{6,5},{7,6},{9,8},{10,9},{11,10},{13,12},{... | collective-permute-start | bytes 442376 | tf_op jit(solution)/shard_map/ppermute | solution.py:22
  39.5 17.8 %slice-start.1 = ((s8[10616832]{0:T(1024)(128)(4,1)}), s8[4194304]{0:T(1024)(128)(4,1)S(1)}, s32[]{:S(2)}) async-start(s8[10616832]{0:T(1024)(128)(4,1)} %bitcast.54), calls=%async_computation.1 | async-start | bytes 8388608
  39.5 17.8 %slice-start.2 = ((s8[10616832]{0:T(1024)(128)(4,1)}), s8[2228224]{0:T(1024)(128)(4,1)S(1)}, s32[]{:S(2)}) async-start(s8[10616832]{0:T(1024)(128)(4,1)} %bitcast.54), calls=%async_computation.2 | async-start | bytes 4456448
  39.6 30.3 %collective-permute-start.5 = (bf16[256,1,288]{0,2,1:T(8,128)(2,1)}, bf16[256,1,288]{0,2,1:T(8,128)(2,1)}, u32[]{:S(2)}, u32[]{:S(2)}) collective-permute-start(bf16[256,1,288]{0,2,1:T(8,128)(2,1)} %get-tuple-element.6), channel_id=1, source_target_pairs={{0,1},{1,2},{2,3},{4,5},{5,6},{6,7},{8,9},{9,10},{10,11},{12,13},{... | collective-permute-start | bytes 442376 | tf_op jit(solution)/shard_map/ppermute | solution.py:20
  69.8 21.9 %copy-start.4 = (bf16[256,8,256]{2,1,0:T(8,128)(2,1)S(1)}, bf16[256,8,256]{2,1,0:T(8,128)(2,1)}, u32[]{:S(2)}) copy-start(bf16[256,8,256]{2,1,0:T(8,128)(2,1)} %param.5) | copy-start | bytes 3145732
  97.2 1.4 copy-start.3
  98.6 3.0 %collective-permute-start.6 = (bf16[1152,256]{1,0:T(8,128)(2,1)S(1)}, bf16[1152,256]{1,0:T(8,128)(2,1)S(1)}, u32[]{:S(2)}, u32[]{:S(2)}) collective-permute-start(bf16[1152,256]{1,0:T(8,128)(2,1)S(1)} %dynamic-slice_convert_fusion), channel_id=1, source_target_pairs={{0,1},{1,0},{2,3},{3,2},{4,5},{5,4},{6,7},{7,6},{8,9},{9,8},{10,11... | collective-permute-start | bytes 1769480 | tf_op jit(solution)/shard_map/ppermute | solution.py:45
  103.0 9.4 %collective-permute-start.7 = (bf16[576,256]{1,0:T(8,128)(2,1)S(1)}, bf16[576,256]{1,0:T(8,128)(2,1)S(1)}, u32[]{:S(2)}, u32[]{:S(2)}) collective-permute-start(bf16[576,256]{1,0:T(8,128)(2,1)S(1)} %dynamic-slice_convert_fusion.1), channel_id=1, source_target_pairs={{0,2},{1,3},{2,0},{3,1},{4,6},{5,7},{6,4},{7,5},{8,10},{9,11},{10,... | collective-permute-start | bytes 884744 | tf_op jit(solution)/shard_map/ppermute | solution.py:45
  112.5 5.3 %collective-permute-start.8 = (bf16[288,256]{1,0:T(8,128)(2,1)S(1)}, bf16[288,256]{1,0:T(8,128)(2,1)S(1)}, u32[]{:S(2)}, u32[]{:S(2)}) collective-permute-start(bf16[288,256]{1,0:T(8,128)(2,1)S(1)} %dynamic-slice_convert_fusion.2), channel_id=1, source_target_pairs={{0,4},{4,0},{8,12},{12,8},{16,20},{20,16},{24,28},{28,24},{1,5},{5... | collective-permute-start | bytes 442376 | tf_op jit(solution)/shard_map/ppermute | solution.py:45
  117.9 4.4 %collective-permute-start.9 = (bf16[144,256]{1,0:T(8,128)(2,1)S(1)}, bf16[144,256]{1,0:T(8,128)(2,1)S(1)}, u32[]{:S(2)}, u32[]{:S(2)}) collective-permute-start(bf16[144,256]{1,0:T(8,128)(2,1)S(1)} %dynamic-slice_convert_fusion.3), channel_id=1, source_target_pairs={{0,8},{4,12},{8,0},{12,4},{16,24},{20,28},{24,16},{28,20},{1,9},{5... | collective-permute-start | bytes 221192 | tf_op jit(solution)/shard_map/ppermute | solution.py:45
  122.3 4.9 %collective-permute-start.10 = (bf16[72,256]{1,0:T(8,128)(2,1)S(1)}, bf16[72,256]{1,0:T(8,128)(2,1)S(1)}, u32[]{:S(2)}, u32[]{:S(2)}) collective-permute-start(bf16[72,256]{1,0:T(8,128)(2,1)S(1)} %dynamic-slice_convert_fusion.4), channel_id=1, source_target_pairs={{0,16},{4,20},{8,24},{12,28},{16,0},{20,4},{24,8},{28,12},{1,17},{... | collective-permute-start | bytes 110600 | tf_op jit(solution)/shard_map/ppermute | solution.py:45
  127.3 5.4 %collective-permute-start.11 = (f32[72,256]{1,0:T(8,128)S(1)}, f32[72,256]{1,0:T(8,128)S(1)}, u32[]{:S(2)}, u32[]{:S(2)}) collective-permute-start(f32[72,256]{1,0:T(8,128)S(1)} %get-tuple-element.5), channel_id=1, source_target_pairs={{0,16},{4,20},{8,24},{12,28},{16,0},{20,4},{24,8},{28,12},{1,17},{... | collective-permute-start | bytes 221192 | tf_op jit(solution)/shard_map/ppermute | solution.py:50
  132.7 5.2 %collective-permute-start.12 = (f32[144,256]{1,0:T(8,128)S(1)}, f32[144,256]{1,0:T(8,128)S(1)}, u32[]{:S(2)}, u32[]{:S(2)}) collective-permute-start(f32[144,256]{1,0:T(8,128)S(1)} %constant_dynamic-update-slice_fusion.8), channel_id=1, source_target_pairs={{0,8},{4,12},{8,0},{12,4},{16,24},{20,28},{24,16},{28,20},{1,9},{5... | collective-permute-start | bytes 442376 | tf_op jit(solution)/shard_map/ppermute | solution.py:50
  138.0 7.4 %collective-permute-start.13 = (f32[288,256]{1,0:T(8,128)S(1)}, f32[288,256]{1,0:T(8,128)S(1)}, u32[]{:S(2)}, u32[]{:S(2)}) collective-permute-start(f32[288,256]{1,0:T(8,128)S(1)} %constant_dynamic-update-slice_fusion.6), channel_id=1, source_target_pairs={{0,4},{4,0},{8,12},{12,8},{16,20},{20,16},{24,28},{28,24},{1,5},{5... | collective-permute-start | bytes 884744 | tf_op jit(solution)/shard_map/ppermute | solution.py:50
  145.4 9.9 %collective-permute-start.14 = (f32[576,256]{1,0:T(8,128)S(1)}, f32[576,256]{1,0:T(8,128)S(1)}, u32[]{:S(2)}, u32[]{:S(2)}) collective-permute-start(f32[576,256]{1,0:T(8,128)S(1)} %constant_dynamic-update-slice_fusion.4), channel_id=1, source_target_pairs={{0,2},{1,3},{2,0},{3,1},{4,6},{5,7},{6,4},{7,5},{8,10},{9,11},{10,... | collective-permute-start | bytes 1769480 | tf_op jit(solution)/shard_map/ppermute | solution.py:50
  155.4 10.3 %collective-permute-start.15 = (f32[1152,256]{1,0:T(8,128)S(1)}, f32[1152,256]{1,0:T(8,128)S(1)}, u32[]{:S(2)}, u32[]{:S(2)}) collective-permute-start(f32[1152,256]{1,0:T(8,128)S(1)} %constant_dynamic-update-slice_fusion.2), channel_id=1, source_target_pairs={{0,1},{1,0},{2,3},{3,2},{4,5},{5,4},{6,7},{7,6},{8,9},{9,8},{10,11... | collective-permute-start | bytes 3538952 | tf_op jit(solution)/shard_map/ppermute | solution.py:50

commit v3 on v2

--- a/solution.py
+++ b/solution.py
@@ -44,6 +44,7 @@
         send = lax.dynamic_slice_in_dim(cur, (1 - side) * half, half, 0)
         sent = lax.ppermute(send.astype(jnp.bfloat16), axis, [(i, i ^ bit) for i in range(count)])
         cur = keep + sent.astype(cur.dtype)
+    cur = cur.astype(jnp.bfloat16)
     for axis, bit in reversed(stages):
         count = lax.axis_size(axis)
         side = (lax.axis_index(axis) // bit) % 2
@@ -52,7 +53,7 @@
         buf = jnp.zeros((2 * half, cur.shape[1]), cur.dtype)
         buf = lax.dynamic_update_slice_in_dim(buf, cur, side * half, 0)
         cur = lax.dynamic_update_slice_in_dim(buf, other, (1 - side) * half, 0)
-    return cur.reshape(x.shape)
+    return cur.astype(x.dtype).reshape(x.shape)
 
 
 def spread_block(source, coef_source, row_first, rows, col_first, cols):

time: 168 us -> 159 us (0.946)
  waiting for transfers between devices: 43.8 us -> 38 us
    ppermute x5, waiting for transfers between devices: 21 us -> 15.2 us  [halving_psum(): other = lax.ppermute(cur, axis, [(i, i ^ bit) for i in range(count)])]
  transfers between devices with their start and end apart: 16 -> 16, of which waited for: 9 -> 9; matrix products, arithmetic and copies ran while one was open for 36% -> 37% of each run, Pallas kernels for 0% -> 0%
where the time goes in v3:
time: 159 us
  matrix products  80.8 us (51%)
  waiting for transfers between devices  38 us (24%)
  starting transfers between devices  26.4 us (17%)
  local copies, waits for them, and re-layouts  6.14 us (4%)
  other arithmetic  6.08 us (4%)
    dot_general x3, matrix products, spread_block(): jnp.einsum('oip,kipq->koiq', rows_in, tiles, preferred_element_type=jnp.f...  47.2 us
    ppermute x5, waiting for transfers between devices, halving_psum(): lax.ppermute(send.astype(jnp.bfloat16), axis, [(i, i ^ bit) for i in rang...  22.8 us
    dot_general x3, matrix products, spread_block(): jnp.einsum('bpq,kib->kipq', selector, part_coefs, preferred_element_type=...  21.8 us
    ppermute x5, waiting for transfers between devices, halving_psum(): other = lax.ppermute(cur, axis, [(i, i ^ bit) for i in range(count)])  15.2 us
    ppermute x3, starting transfers between devices, with_halo(): lax.ppermute(head, axis, [((i + 1) % count, i) for i in range(ends)])  8.76 us
    ppermute x3, starting transfers between devices, with_halo(): lax.ppermute(tail, axis, [(i, (i + 1) % count) for i in range(ends)])  7.63 us
    dot_general x1, matrix products, local(): jnp.einsum('koc,koiq->ciq', mixing, spread, preferred_element_type=jnp.fl...  6.3 us
    ppermute x5, starting transfers between devices, halving_psum(): other = lax.ppermute(cur, axis, [(i, i ^ bit) for i in range(count)])  5.94 us
  transfers between devices with their start and end apart: 16, of which 9 were waited for; matrix products, arithmetic and copies ran while one was open for 37% of the time, Pallas kernels for 0%

profile of v3, /device:TPU:0, one launch (start us, length us, event | category | flops | bytes accessed | tf_op | source)
XLA Modules:
  0.0 158.6 jit_solution(13045001593559182984)
XLA Ops:
  0.6 0.0 copy-start
  0.7 0.8 compare_convert_fusion
  1.5 0.8 broadcast_multiply_fusion
  2.3 1.3 collective-permute-start
  3.6 1.6 %copy.7 = bf16[256,8,256]{0,2,1:T(8,128)(2,1)S(1)} copy(bf16[256,8,256]{2,1,0:T(8,128)(2,1)} %param.6) | data formatting | bytes 2097152 | tf_op args[1]
  5.3 6.1 %collective-permute-start.2 = (bf16[256,8,16]{0,2,1:T(8,128)(2,1)S(1)}, bf16[256,8,16]{0,2,1:T(8,128)(2,1)S(1)}, u32[]{:S(2)}, u32[]{:S(2)}) collective-permute-start(bf16[256,8,16]{0,2,1:T(8,128)(2,1)S(1)} %get-tuple-element.9), channel_id=1, source_target_pairs={{4,0},{8,4},{12,8},{16,12},{20,16},{24,20},{28,24},{0,28},{5,1},{9... | collective-permute-start | bytes 196616 | tf_op jit(solution)/shard_map/ppermute | solution.py:22
  11.4 0.0 collective-permute-start.1
  11.4 2.7 %collective-permute-start.4 = (bf16[9,1,3,33]{3,1,2,0:T(2,128)(2,1)S(1)}, bf16[9,1,3,33]{3,1,2,0:T(2,128)(2,1)S(1)}, u32[]{:S(2)}, u32[]{:S(2)}) collective-permute-start(bf16[9,1,3,33]{3,1,2,0:T(2,128)(2,1)S(1)} %get-tuple-element.10), channel_id=1, source_target_pairs={{0,1},{1,2},{2,3},{4,5},{5,6},{6,7},{8,9},{9,10},{10,11},{12,13},{... | collective-permute-start | bytes 5354 | tf_op jit(solution)/shard_map/ppermute | solution.py:20
  14.1 1.3 fusion.3
  15.4 0.0 copy-start.1
  15.4 6.6 %fusion.7 = bf16[9,8,288,256]{3,1,2,0:T(8,128)(2,1)} fusion(pred[33,288,256,1]{2,1,0,3:T(32,128)(4,1)S(1)} %fusion.3, bf16[9,8,3,33]{3,1,2,0:T(8,128)(2,1)S(1)} %broadcast_multiply_fusion), kind=kOutput, calls=%fused_computation.12 | convolution fusion | flops 350355456 | bytes 13068288 | tf_op jit(solution)/shard_map/bpq,kib->kipq/dot_general | solution.py:75
  22.0 0.0 copy-done.1
  22.0 0.0 collective-permute-done
  22.0 8.6 %fusion.9 = bf16[9,8,288,256]{3,1,2,0:T(8,128)(2,1)} fusion(pred[33,288,256,1]{2,1,0,3:T(32,128)(4,1)} %copy-done.1, bf16[9,1,3,33]{3,1,2,0:T(2,128)(2,1)S(1)} %collective-permute-done, bf16[9,8,3,33]{3,1,2,0:T(8,128)(2,1)S(1)} %broadcast_multiply_fusion), kind=kOutput, calls=%fused_computation.14 | convolution fusion | flops 350364960 | bytes 13065894 | tf_op jit(solution)/shard_map/bpq,kib->kipq/dot_general | solution.py:75
  30.6 0.0 collective-permute-done.4
  30.6 0.0 copy-done.2
  30.6 6.6 %fusion.5 = bf16[9,8,288,256]{3,1,2,0:T(8,128)(2,1)} fusion(pred[33,288,256,1]{2,1,0,3:T(32,128)(4,1)S(1)} %copy-done.2, bf16[9,8,3,33]{3,1,2,0:T(8,128)(2,1)S(1)} %broadcast_multiply_fusion, bf16[9,1,3,33]{3,1,2,0:T(2,128)(2,1)S(1)} %collective-permute-done.4), kind=kOutput, calls=%fused_computation.10 | convolution fusion | flops 350364960 | bytes 13065894 | tf_op jit(solution)/shard_map/bpq,kib->kipq/dot_general | solution.py:75
  37.3 0.0 collective-permute-done.2
  37.3 0.0 collective-permute-done.1
  37.3 0.1 pad_maximum_fusion.10
  37.4 0.0 slice-start
  37.4 0.7 fusion.32
  38.1 1.4 collective-permute-start.3
  39.5 0.0 slice-start.1
  39.5 0.0 slice-start.2
  39.6 4.9 %collective-permute-start.5 = (bf16[256,1,288]{0,2,1:T(8,128)(2,1)}, bf16[256,1,288]{0,2,1:T(8,128)(2,1)}, u32[]{:S(2)}, u32[]{:S(2)}) collective-permute-start(bf16[256,1,288]{0,2,1:T(8,128)(2,1)} %get-tuple-element.6), channel_id=1, source_target_pairs={{0,1},{1,2},{2,3},{4,5},{5,6},{6,7},{8,9},{9,10},{10,11},{12,13},{... | collective-permute-start | bytes 442376 | tf_op jit(solution)/shard_map/ppermute | solution.py:20
  44.4 12.9 %fusion.1 = f32[8,9,256,256]{3,2,1,0:T(8,128)} fusion(bf16[9,8,288,256]{3,1,2,0:T(8,128)(2,1)} %fusion.7, bf16[256,8,16]{0,2,1:T(8,128)(2,1)S(1)} %collective-permute-done.2, bf16[256,8,256]{0,2,1:T(8,128)(2,1)S(1)} %copy.7, bf16[256,8,16]{0,2,1:T(8,128)(2,1)S(1)} %collective-permute-done.1), kind=kOutput, calls=%fused_computation.5 | convolution fusion | flops 2721447936 | bytes 30670848 | tf_op jit(solution)/shard_map/oip,kipq->koiq/dot_general | solution.py:78
  57.4 0.0 collective-permute-done.3
  57.4 0.0 slice-done
  57.4 0.0 slice-done.1
  57.4 0.0 slice-done.2
  57.4 12.4 %fusion = f32[8,9,256,256]{3,2,1,0:T(8,128)} fusion(bf16[9,8,288,256]{3,1,2,0:T(8,128)(2,1)S(1)} %bitcast.55, bf16[256,1,288]{0,2,1:T(8,128)(2,1)} %collective-permute-done.3, bf16[256,8,16]{0,2,1:T(8,128)(2,1)S(1)} %collective-permute-done.2, bf16[256,8,256]{0,2,1:T(8,128)(2,1)S(1)} %copy.7, bf16[256,8,16]{0,2,1:T(8,128)(2,1)S(1)} %collective-permute-done.1), kind=kOutput, calls=%fused_computation.4 | convolution fusion | flops 2722627584 | bytes 30818304 | tf_op jit(solution)/shard_map/oip,kipq->koiq/dot_general | solution.py:78
  69.8 0.0 collective-permute-done.5
  69.8 21.9 %fusion.4 = bf16[9,256,8,256]{1,3,0,2:T(8,128)(2,1)} fusion(f32[8,9,256,256]{3,2,1,0:T(8,128)} %fusion, f32[8,9,256,256]{3,2,1,0:T(8,128)} %fusion.1, bf16[9,8,288,256]{3,1,2,0:T(8,128)(2,1)} %fusion.5, bf16[256,1,288]{0,2,1:T(8,128)(2,1)} %collective-permute-done.5, bf16[256,8,16]{0,2,1:T(8,128)(2,1)S(1)} %collective-permute-done.2, ...), kind=kOutput, calls=%fused_computation.9 | convolution fusion | flops 2736783360 | bytes 59129856 | tf_op jit(solution)/shard_map/oip,kipq->koiq/dot_general | solution.py:78
  91.7 5.5 %fusion.20 = f32[9,256,256,1]{2,1,0,3:T(8,128)S(1)} fusion(bf16[9,256,8,256]{1,3,0,2:T(8,128)(2,1)} %fusion.4, bf16[256,8,256,1]{2,1,0,3:T(8,128)(2,1)S(1)} %bitcast.59), kind=kOutput, calls=%fused_computation.34 | convolution fusion | flops 2415919104 | bytes 12845056 | tf_op jit(solution)/shard_map/koiq,ciq->koc/dot_general | solution.py:96
  97.2 0.0 copy-start.3
  97.2 1.4 copy-done.3
  98.6 0.1 dynamic-slice_convert_fusion
  98.6 1.3 collective-permute-start.6
  100.0 1.6 %collective-permute-done.6 = bf16[1152,256]{1,0:T(8,128)(2,1)S(1)} collective-permute-done((bf16[1152,256]{1,0:T(8,128)(2,1)S(1)}, bf16[1152,256]{1,0:T(8,128)(2,1)S(1)}, u32[]{:S(2)}, u32[]{:S(2)}) %collective-permute-start.6) | collective-permute-done | bytes 589856 | tf_op jit(solution)/shard_map/ppermute | solution.py:45
  101.6 1.4 convert_add_fusion
  103.0 0.5 collective-permute-start.7
  103.5 8.9 %collective-permute-done.7 = bf16[576,256]{1,0:T(8,128)(2,1)S(1)} collective-permute-done((bf16[576,256]{1,0:T(8,128)(2,1)S(1)}, bf16[576,256]{1,0:T(8,128)(2,1)S(1)}, u32[]{:S(2)}, u32[]{:S(2)}) %collective-permute-start.7) | collective-permute-done | bytes 294944 | tf_op jit(solution)/shard_map/ppermute | solution.py:45
  112.4 0.1 convert_add_fusion.1
  112.5 0.1 collective-permute-start.8
  112.6 5.2 %collective-permute-done.8 = bf16[288,256]{1,0:T(8,128)(2,1)S(1)} collective-permute-done((bf16[288,256]{1,0:T(8,128)(2,1)S(1)}, bf16[288,256]{1,0:T(8,128)(2,1)S(1)}, u32[]{:S(2)}, u32[]{:S(2)}) %collective-permute-start.8) | collective-permute-done | bytes 147488 | tf_op jit(solution)/shard_map/ppermute | solution.py:45
  117.9 0.1 collective-permute-start.9
  118.0 4.3 %collective-permute-done.9 = bf16[144,256]{1,0:T(8,128)(2,1)S(1)} collective-permute-done((bf16[144,256]{1,0:T(8,128)(2,1)S(1)}, bf16[144,256]{1,0:T(8,128)(2,1)S(1)}, u32[]{:S(2)}, u32[]{:S(2)}) %collective-permute-start.9) | collective-permute-done | bytes 73760 | tf_op jit(solution)/shard_map/ppermute | solution.py:45
  122.3 2.2 %collective-permute-start.10 = (bf16[72,256]{1,0:T(8,128)(2,1)S(1)}, bf16[72,256]{1,0:T(8,128)(2,1)S(1)}, u32[]{:S(2)}, u32[]{:S(2)}) collective-permute-start(bf16[72,256]{1,0:T(8,128)(2,1)S(1)} %dynamic-slice_convert_fusion.4), channel_id=1, source_target_pairs={{0,16},{4,20},{8,24},{12,28},{16,0},{20,4},{24,8},{28,12},{1,17},{... | collective-permute-start | bytes 110600 | tf_op jit(solution)/shard_map/ppermute | solution.py:45
  124.5 2.8 %collective-permute-done.10 = bf16[72,256]{1,0:T(8,128)(2,1)S(1)} collective-permute-done((bf16[72,256]{1,0:T(8,128)(2,1)S(1)}, bf16[72,256]{1,0:T(8,128)(2,1)S(1)}, u32[]{:S(2)}, u32[]{:S(2)}) %collective-permute-start.10) | collective-permute-done | bytes 36896 | tf_op jit(solution)/shard_map/ppermute | solution.py:45
  127.3 2.2 %collective-permute-start.11 = (bf16[72,256]{1,0:T(8,128)(2,1)S(1)}, bf16[72,256]{1,0:T(8,128)(2,1)S(1)}, u32[]{:S(2)}, u32[]{:S(2)}) collective-permute-start(bf16[72,256]{1,0:T(8,128)(2,1)S(1)} %get-tuple-element.5), channel_id=1, source_target_pairs={{0,16},{4,20},{8,24},{12,28},{16,0},{20,4},{24,8},{28,12},{1,17},{... | collective-permute-start | bytes 110600 | tf_op jit(solution)/shard_map/ppermute | solution.py:51
  129.5 2.8 %collective-permute-done.11 = bf16[72,256]{1,0:T(8,128)(2,1)S(1)} collective-permute-done((bf16[72,256]{1,0:T(8,128)(2,1)S(1)}, bf16[72,256]{1,0:T(8,128)(2,1)S(1)}, u32[]{:S(2)}, u32[]{:S(2)}) %collective-permute-start.11) | collective-permute-done | bytes 36896 | tf_op jit(solution)/shard_map/ppermute | solution.py:51
  132.2 1.7 %collective-permute-start.12 = (bf16[144,256]{1,0:T(8,128)(2,1)S(1)}, bf16[144,256]{1,0:T(8,128)(2,1)S(1)}, u32[]{:S(2)}, u32[]{:S(2)}) collective-permute-start(bf16[144,256]{1,0:T(8,128)(2,1)S(1)} %constant_dynamic-update-slice_fusion.8), channel_id=1, source_target_pairs={{0,8},{4,12},{8,0},{12,4},{16,24},{20,28},{24,16},{28,20},{1,9},{5... | collective-permute-start | bytes 221192 | tf_op jit(solution)/shard_map/ppermute | solution.py:51
  133.9 2.6 %collective-permute-done.12 = bf16[144,256]{1,0:T(8,128)(2,1)S(1)} collective-permute-done((bf16[144,256]{1,0:T(8,128)(2,1)S(1)}, bf16[144,256]{1,0:T(8,128)(2,1)S(1)}, u32[]{:S(2)}, u32[]{:S(2)}) %collective-permute-start.12) | collective-permute-done | bytes 73760 | tf_op jit(solution)/shard_map/ppermute | solution.py:51
  136.6 1.7 %collective-permute-start.13 = (bf16[288,256]{1,0:T(8,128)(2,1)S(1)}, bf16[288,256]{1,0:T(8,128)(2,1)S(1)}, u32[]{:S(2)}, u32[]{:S(2)}) collective-permute-start(bf16[288,256]{1,0:T(8,128)(2,1)S(1)} %constant_dynamic-update-slice_fusion.6), channel_id=1, source_target_pairs={{0,4},{4,0},{8,12},{12,8},{16,20},{20,16},{24,28},{28,24},{1,5},{5... | collective-permute-start | bytes 442376 | tf_op jit(solution)/shard_map/ppermute | solution.py:51
  138.3 3.4 %collective-permute-done.13 = bf16[288,256]{1,0:T(8,128)(2,1)S(1)} collective-permute-done((bf16[288,256]{1,0:T(8,128)(2,1)S(1)}, bf16[288,256]{1,0:T(8,128)(2,1)S(1)}, u32[]{:S(2)}, u32[]{:S(2)}) %collective-permute-start.13) | collective-permute-done | bytes 147488 | tf_op jit(solution)/shard_map/ppermute | solution.py:51
  141.8 0.3 collective-permute-start.14
  142.2 6.4 %collective-permute-done.14 = bf16[576,256]{1,0:T(8,128)(2,1)S(1)} collective-permute-done((bf16[576,256]{1,0:T(8,128)(2,1)S(1)}, bf16[576,256]{1,0:T(8,128)(2,1)S(1)}, u32[]{:S(2)}, u32[]{:S(2)}) %collective-permute-start.14) | collective-permute-done | bytes 294944 | tf_op jit(solution)/shard_map/ppermute | solution.py:51
  148.6 0.1 collective-permute-start.15
  148.7 6.3 %fusion.11 = bf16[256,8,256]{0,2,1:T(8,128)(2,1)S(1)} fusion(bf16[9,256,8,256]{1,3,0,2:T(8,128)(2,1)} %fusion.4, bf16[9,256,256]{2,1,0:T(8,128)(2,1)S(1)} %copy-done), kind=kOutput, calls=%fused_computation.18 | convolution fusion | flops 2416443392 | bytes 11665408 | tf_op jit(solution)/shard_map/koc,koiq->ciq/dot_general | solution.py:99
  155.0 1.8 %copy.12 = bf16[256,8,256]{2,1,0:T(8,128)(2,1)} copy(bf16[256,8,256]{0,2,1:T(8,128)(2,1)S(1)} %fusion.11) | data formatting | bytes 2097152
  156.8 0.1 broadcast_in_dim.10
  157.0 0.0 collective-permute-done.15
  157.0 1.6 convert_multiply_fusion
  (30 shorter events, 0.5 us)
Async XLA Ops:
  0.6 148.1 %copy-start = (bf16[9,256,256]{2,1,0:T(8,128)(2,1)S(1)}, bf16[9,256,256]{2,1,0:T(8,128)(2,1)}, u32[]{:S(2)}) copy-start(bf16[9,256,256]{2,1,0:T(8,128)(2,1)} %param.7) | copy-start | bytes 3538948
  2.3 19.7 %collective-permute-start = (bf16[9,1,3,33]{3,1,2,0:T(2,128)(2,1)S(1)}, bf16[9,1,3,33]{3,1,2,0:T(2,128)(2,1)S(1)}, u32[]{:S(2)}, u32[]{:S(2)}) collective-permute-start(bf16[9,1,3,33]{3,1,2,0:T(2,128)(2,1)S(1)} %get-tuple-element.11), channel_id=1, source_target_pairs={{1,0},{2,1},{3,2},{5,4},{6,5},{7,6},{9,8},{10,9},{11,10},{13,12},{... | collective-permute-start | bytes 5354 | tf_op jit(solution)/shard_map/ppermute | solution.py:22
  5.3 32.0 %collective-permute-start.2 = (bf16[256,8,16]{0,2,1:T(8,128)(2,1)S(1)}, bf16[256,8,16]{0,2,1:T(8,128)(2,1)S(1)}, u32[]{:S(2)}, u32[]{:S(2)}) collective-permute-start(bf16[256,8,16]{0,2,1:T(8,128)(2,1)S(1)} %get-tuple-element.9), channel_id=1, source_target_pairs={{4,0},{8,4},{12,8},{16,12},{20,16},{24,20},{28,24},{0,28},{5,1},{9... | collective-permute-start | bytes 196616 | tf_op jit(solution)/shard_map/ppermute | solution.py:22
  11.4 25.9 %collective-permute-start.1 = (bf16[256,8,16]{0,2,1:T(8,128)(2,1)S(1)}, bf16[256,8,16]{0,2,1:T(8,128)(2,1)S(1)}, u32[]{:S(2)}, u32[]{:S(2)}) collective-permute-start(bf16[256,8,16]{0,2,1:T(8,128)(2,1)S(1)} %get-tuple-element.8), channel_id=1, source_target_pairs={{0,4},{4,8},{8,12},{12,16},{16,20},{20,24},{24,28},{28,0},{1,5},{5... | collective-permute-start | bytes 196616 | tf_op jit(solution)/shard_map/ppermute | solution.py:20
  11.4 19.3 %collective-permute-start.4 = (bf16[9,1,3,33]{3,1,2,0:T(2,128)(2,1)S(1)}, bf16[9,1,3,33]{3,1,2,0:T(2,128)(2,1)S(1)}, u32[]{:S(2)}, u32[]{:S(2)}) collective-permute-start(bf16[9,1,3,33]{3,1,2,0:T(2,128)(2,1)S(1)} %get-tuple-element.10), channel_id=1, source_target_pairs={{0,1},{1,2},{2,3},{4,5},{5,6},{6,7},{8,9},{9,10},{10,11},{12,13},{... | collective-permute-start | bytes 5354 | tf_op jit(solution)/shard_map/ppermute | solution.py:20
  15.4 6.6 %copy-start.1 = (pred[33,288,256,1]{2,1,0,3:T(32,128)(4,1)}, pred[33,288,256,1]{2,1,0,3:T(32,128)(4,1)S(1)}, u32[]{:S(2)}) copy-start(pred[33,288,256,1]{2,1,0,3:T(32,128)(4,1)S(1)} %fusion.3) | copy-start | bytes 7299076
  22.0 8.6 %copy-start.2 = (pred[33,288,256,1]{2,1,0,3:T(32,128)(4,1)S(1)}, pred[33,288,256,1]{2,1,0,3:T(32,128)(4,1)}, u32[]{:S(2)}) copy-start(pred[33,288,256,1]{2,1,0,3:T(32,128)(4,1)} %copy-done.1) | copy-start | bytes 7299076
  37.4 20.0 %slice-start = ((s8[10616832]{0:T(1024)(128)(4,1)}), s8[4194304]{0:T(1024)(128)(4,1)S(1)}, s32[]{:S(2)}) async-start(s8[10616832]{0:T(1024)(128)(4,1)} %bitcast.54), calls=%async_computation | async-start | bytes 8388608
  38.1 19.2 %collective-permute-start.3 = (bf16[256,1,288]{0,2,1:T(8,128)(2,1)}, bf16[256,1,288]{0,2,1:T(8,128)(2,1)}, u32[]{:S(2)}, u32[]{:S(2)}) collective-permute-start(bf16[256,1,288]{0,2,1:T(8,128)(2,1)} %get-tuple-element.7), channel_id=1, source_target_pairs={{1,0},{2,1},{3,2},{5,4},{6,5},{7,6},{9,8},{10,9},{11,10},{13,12},{... | collective-permute-start | bytes 442376 | tf_op jit(solution)/shard_map/ppermute | solution.py:22
  39.5 17.8 %slice-start.1 = ((s8[10616832]{0:T(1024)(128)(4,1)}), s8[4194304]{0:T(1024)(128)(4,1)S(1)}, s32[]{:S(2)}) async-start(s8[10616832]{0:T(1024)(128)(4,1)} %bitcast.54), calls=%async_computation.1 | async-start | bytes 8388608
  39.5 17.8 %slice-start.2 = ((s8[10616832]{0:T(1024)(128)(4,1)}), s8[2228224]{0:T(1024)(128)(4,1)S(1)}, s32[]{:S(2)}) async-start(s8[10616832]{0:T(1024)(128)(4,1)} %bitcast.54), calls=%async_computation.2 | async-start | bytes 4456448
  39.6 30.3 %collective-permute-start.5 = (bf16[256,1,288]{0,2,1:T(8,128)(2,1)}, bf16[256,1,288]{0,2,1:T(8,128)(2,1)}, u32[]{:S(2)}, u32[]{:S(2)}) collective-permute-start(bf16[256,1,288]{0,2,1:T(8,128)(2,1)} %get-tuple-element.6), channel_id=1, source_target_pairs={{0,1},{1,2},{2,3},{4,5},{5,6},{6,7},{8,9},{9,10},{10,11},{12,13},{... | collective-permute-start | bytes 442376 | tf_op jit(solution)/shard_map/ppermute | solution.py:20
  69.8 21.9 %copy-start.4 = (bf16[256,8,256]{2,1,0:T(8,128)(2,1)S(1)}, bf16[256,8,256]{2,1,0:T(8,128)(2,1)}, u32[]{:S(2)}) copy-start(bf16[256,8,256]{2,1,0:T(8,128)(2,1)} %param.5) | copy-start | bytes 3145732
  97.2 1.4 copy-start.3
  98.6 3.0 %collective-permute-start.6 = (bf16[1152,256]{1,0:T(8,128)(2,1)S(1)}, bf16[1152,256]{1,0:T(8,128)(2,1)S(1)}, u32[]{:S(2)}, u32[]{:S(2)}) collective-permute-start(bf16[1152,256]{1,0:T(8,128)(2,1)S(1)} %dynamic-slice_convert_fusion), channel_id=1, source_target_pairs={{0,1},{1,0},{2,3},{3,2},{4,5},{5,4},{6,7},{7,6},{8,9},{9,8},{10,11... | collective-permute-start | bytes 1769480 | tf_op jit(solution)/shard_map/ppermute | solution.py:45
  103.0 9.4 %collective-permute-start.7 = (bf16[576,256]{1,0:T(8,128)(2,1)S(1)}, bf16[576,256]{1,0:T(8,128)(2,1)S(1)}, u32[]{:S(2)}, u32[]{:S(2)}) collective-permute-start(bf16[576,256]{1,0:T(8,128)(2,1)S(1)} %dynamic-slice_convert_fusion.1), channel_id=1, source_target_pairs={{0,2},{1,3},{2,0},{3,1},{4,6},{5,7},{6,4},{7,5},{8,10},{9,11},{10,... | collective-permute-start | bytes 884744 | tf_op jit(solution)/shard_map/ppermute | solution.py:45
  112.5 5.3 %collective-permute-start.8 = (bf16[288,256]{1,0:T(8,128)(2,1)S(1)}, bf16[288,256]{1,0:T(8,128)(2,1)S(1)}, u32[]{:S(2)}, u32[]{:S(2)}) collective-permute-start(bf16[288,256]{1,0:T(8,128)(2,1)S(1)} %dynamic-slice_convert_fusion.2), channel_id=1, source_target_pairs={{0,4},{4,0},{8,12},{12,8},{16,20},{20,16},{24,28},{28,24},{1,5},{5... | collective-permute-start | bytes 442376 | tf_op jit(solution)/shard_map/ppermute | solution.py:45
  117.9 4.4 %collective-permute-start.9 = (bf16[144,256]{1,0:T(8,128)(2,1)S(1)}, bf16[144,256]{1,0:T(8,128)(2,1)S(1)}, u32[]{:S(2)}, u32[]{:S(2)}) collective-permute-start(bf16[144,256]{1,0:T(8,128)(2,1)S(1)} %dynamic-slice_convert_fusion.3), channel_id=1, source_target_pairs={{0,8},{4,12},{8,0},{12,4},{16,24},{20,28},{24,16},{28,20},{1,9},{5... | collective-permute-start | bytes 221192 | tf_op jit(solution)/shard_map/ppermute | solution.py:45
  122.3 4.9 %collective-permute-start.10 = (bf16[72,256]{1,0:T(8,128)(2,1)S(1)}, bf16[72,256]{1,0:T(8,128)(2,1)S(1)}, u32[]{:S(2)}, u32[]{:S(2)}) collective-permute-start(bf16[72,256]{1,0:T(8,128)(2,1)S(1)} %dynamic-slice_convert_fusion.4), channel_id=1, source_target_pairs={{0,16},{4,20},{8,24},{12,28},{16,0},{20,4},{24,8},{28,12},{1,17},{... | collective-permute-start | bytes 110600 | tf_op jit(solution)/shard_map/ppermute | solution.py:45
  127.3 4.9 %collective-permute-start.11 = (bf16[72,256]{1,0:T(8,128)(2,1)S(1)}, bf16[72,256]{1,0:T(8,128)(2,1)S(1)}, u32[]{:S(2)}, u32[]{:S(2)}) collective-permute-start(bf16[72,256]{1,0:T(8,128)(2,1)S(1)} %get-tuple-element.5), channel_id=1, source_target_pairs={{0,16},{4,20},{8,24},{12,28},{16,0},{20,4},{24,8},{28,12},{1,17},{... | collective-permute-start | bytes 110600 | tf_op jit(solution)/shard_map/ppermute | solution.py:51
  132.2 4.4 %collective-permute-start.12 = (bf16[144,256]{1,0:T(8,128)(2,1)S(1)}, bf16[144,256]{1,0:T(8,128)(2,1)S(1)}, u32[]{:S(2)}, u32[]{:S(2)}) collective-permute-start(bf16[144,256]{1,0:T(8,128)(2,1)S(1)} %constant_dynamic-update-slice_fusion.8), channel_id=1, source_target_pairs={{0,8},{4,12},{8,0},{12,4},{16,24},{20,28},{24,16},{28,20},{1,9},{5... | collective-permute-start | bytes 221192 | tf_op jit(solution)/shard_map/ppermute | solution.py:51
  136.6 5.2 %collective-permute-start.13 = (bf16[288,256]{1,0:T(8,128)(2,1)S(1)}, bf16[288,256]{1,0:T(8,128)(2,1)S(1)}, u32[]{:S(2)}, u32[]{:S(2)}) collective-permute-start(bf16[288,256]{1,0:T(8,128)(2,1)S(1)} %constant_dynamic-update-slice_fusion.6), channel_id=1, source_target_pairs={{0,4},{4,0},{8,12},{12,8},{16,20},{20,16},{24,28},{28,24},{1,5},{5... | collective-permute-start | bytes 442376 | tf_op jit(solution)/shard_map/ppermute | solution.py:51
  141.8 6.8 %collective-permute-start.14 = (bf16[576,256]{1,0:T(8,128)(2,1)S(1)}, bf16[576,256]{1,0:T(8,128)(2,1)S(1)}, u32[]{:S(2)}, u32[]{:S(2)}) collective-permute-start(bf16[576,256]{1,0:T(8,128)(2,1)S(1)} %constant_dynamic-update-slice_fusion.4), channel_id=1, source_target_pairs={{0,2},{1,3},{2,0},{3,1},{4,6},{5,7},{6,4},{7,5},{8,10},{9,11},{10,... | collective-permute-start | bytes 884744 | tf_op jit(solution)/shard_map/ppermute | solution.py:51
  148.6 8.3 %collective-permute-start.15 = (bf16[1152,256]{1,0:T(8,128)(2,1)S(1)}, bf16[1152,256]{1,0:T(8,128)(2,1)S(1)}, u32[]{:S(2)}, u32[]{:S(2)}) collective-permute-start(bf16[1152,256]{1,0:T(8,128)(2,1)S(1)} %constant_dynamic-update-slice_fusion.2), channel_id=1, source_target_pairs={{0,1},{1,0},{2,3},{3,2},{4,5},{5,4},{6,7},{7,6},{8,9},{9,8},{10,11... | collective-permute-start | bytes 1769480 | tf_op jit(solution)/shard_map/ppermute | solution.py:51
